TPU v7x, 32 devices: a whole 2x2x4 slice. The times are simulated.
32 devices in a mesh: fsdp: 32 (over z, y, x, core).
Axes of the slice: x: 2, y: 2, z: 4, core: 2. Of those that a mesh axis runs over, the one named last changes fastest.
Arguments:
- block_input: bfloat16 [32, 196, 512], P('fsdp'), may hold values from -6 to 6
- out_cotangent: bfloat16 [32, 196, 512], P('fsdp'), may hold values from -6 to 6
- norm1_gain: bfloat16 [512], P('fsdp'), may hold values from 0.099609375 to 1.8984375
- norm1_bias: bfloat16 [512], P('fsdp'), may hold values from -3 to 3
- qkv_weight: bfloat16 [512, 1536], P('fsdp'), may hold values from -0.25 to 0.25
- qv_bias: bfloat16 [1024], P('fsdp'), may hold values from -3 to 3
- proj_weight: bfloat16 [512, 512], P('fsdp'), may hold values from -1 to 1
- proj_bias: bfloat16 [512], P('fsdp'), may hold values from -3 to 3
- norm2_gain: bfloat16 [512], P('fsdp'), may hold values from 0.099609375 to 1.8984375
- norm2_bias: bfloat16 [512], P('fsdp'), may hold values from -3 to 3
- fc1_weight: bfloat16 [512, 2048], P('fsdp'), may hold values from -0.25 to 0.25
- fc1_bias: bfloat16 [2048], P('fsdp'), may hold values from -3 to 3
- fc2_weight: bfloat16 [2048, 512], P(None, 'fsdp'), may hold values from -0.125 to 0.125
- fc2_bias: bfloat16 [512], P('fsdp'), may hold values from -3 to 3
- bias_table: bfloat16 [169, 16], replicated, may hold values from -4 to 296
- window_mask: int32 [4, 49, 49], replicated, may hold values from 0 to 1, as said below
- rel_index: int32 [49, 49], replicated, may hold values from 0 to 168
- partition: int32 [196], replicated, may hold values from 0 to 195, each once
Outputs:
- block_output: bfloat16 [32, 196, 512], P('fsdp')
- input_grad: float32 [32, 196, 512], P('fsdp')
- norm1_gain_grad: float32 [512], P('fsdp')
- norm1_bias_grad: float32 [512], P('fsdp')
- qkv_weight_grad: float32 [512, 1536], P('fsdp')
- qv_bias_grad: float32 [1024], P('fsdp')
- proj_weight_grad: float32 [512, 512], P('fsdp')
- proj_bias_grad: float32 [512], P('fsdp')
- norm2_gain_grad: float32 [512], P('fsdp')
- norm2_bias_grad: float32 [512], P('fsdp')
- fc1_weight_grad: float32 [512, 2048], P('fsdp')
- fc1_bias_grad: float32 [2048], P('fsdp')
- fc2_weight_grad: float32 [2048, 512], P(None, 'fsdp')
- fc2_bias_grad: float32 [512], P('fsdp')
- bias_table_grad: float32 [169, 16], replicated
Inputs may be any that keep to these rules, and one draw needn't show every extreme that they name: window_mask[w, i, j] is 1 exactly where positions i and j of window w carry the same region label; it is symmetric and 1 on the diagonal. `partition`: a permutation of 0 to 195.
All inputs are finite; a program needn't handle non-finite values.
Results may differ from a plain program's by a relative error of at most 0.011.
Values may be sent and summed in bfloat16 or wider, within the bound.
A program may use at most 128 MiB of HBM per device.

v0:
```python
import jax
import jax.numpy as jnp
from jax import lax
from jax.sharding import PartitionSpec as P

HEADS = 16
WINDOW = 49
WIN_IMG = 4
MICRO = 1


EPSILON = 1e-05
NEG_FILL = -1e30
ROOT_HALF = 0.7071067811865476
DENSITY = 0.3989422804014327


def normalize(values, gain_vec, shift_vec):
    center = values - jnp.mean(values, axis=-1, keepdims=True)
    inv_std = lax.rsqrt(jnp.mean(center * center, axis=-1, keepdims=True) + EPSILON)
    unit_rows = center * inv_std
    return (unit_rows * gain_vec + shift_vec, unit_rows, inv_std)


def norm_backward(grad_out, unit_rows, inv_std, gain_vec):
    scaled = grad_out * gain_vec
    grad_in = inv_std * (
        scaled
        - jnp.mean(scaled, axis=-1, keepdims=True)
        - unit_rows * jnp.mean(scaled * unit_rows, axis=-1, keepdims=True)
    )
    return (grad_in, jnp.sum(grad_out * unit_rows, axis=0), jnp.sum(grad_out, axis=0))


def gelu_parts(pre_act):
    normal_cdf = 0.5 * (1.0 + jax.scipy.special.erf(pre_act * ROOT_HALF))
    normal_pdf = jnp.exp(-0.5 * pre_act * pre_act) * DENSITY
    return (pre_act * normal_cdf, normal_cdf + pre_act * normal_pdf)


def to_windows(token_rows, partition):
    picked = jnp.take(token_rows, partition, axis=1)
    return picked.reshape(token_rows.shape[0], WIN_IMG, WINDOW, token_rows.shape[-1])


def from_windows(window_rows, inverse):
    flat_rows = window_rows.reshape(window_rows.shape[0], inverse.shape[0], window_rows.shape[-1])
    return jnp.take(flat_rows, inverse, axis=1)


def window_scores(queries, key_rows, lookups, score_scale):
    table_bias, allowed, partition, inverse = lookups
    raw = (
        jnp.einsum("bwihe,bwjhe->bwhij", queries, key_rows, preferred_element_type=jnp.float32)
        * score_scale
        + table_bias
    )
    return jnp.where(allowed, raw, NEG_FILL)


def fetch_pass_fwd(shards):
    return (
        lax.all_gather(shards[0], "fsdp", axis=0, tiled=True),
        lax.all_gather(shards[1], "fsdp", axis=0, tiled=True),
        lax.all_gather(shards[2], "fsdp", axis=0, tiled=True),
        lax.all_gather(shards[3], "fsdp", axis=0, tiled=True),
        lax.all_gather(shards[4], "fsdp", axis=0, tiled=True),
        lax.all_gather(shards[5], "fsdp", axis=0, tiled=True),
        lax.all_gather(shards[6], "fsdp", axis=0, tiled=True),
        lax.all_gather(shards[7], "fsdp", axis=0, tiled=True),
        lax.all_gather(shards[8], "fsdp", axis=0, tiled=True),
        lax.all_gather(shards[9], "fsdp", axis=0, tiled=True),
        lax.all_gather(shards[10], "fsdp", axis=1, tiled=True),
        lax.all_gather(shards[11], "fsdp", axis=0, tiled=True),
    )


def fetch_pass_bwd(shards):
    return (
        lax.all_gather(shards[0], "fsdp", axis=0, tiled=True),
        lax.all_gather(shards[1], "fsdp", axis=0, tiled=True),
        lax.all_gather(shards[2], "fsdp", axis=0, tiled=True),
        lax.all_gather(shards[3], "fsdp", axis=0, tiled=True),
        lax.all_gather(shards[4], "fsdp", axis=0, tiled=True),
        lax.all_gather(shards[5], "fsdp", axis=0, tiled=True),
        lax.all_gather(shards[6], "fsdp", axis=0, tiled=True),
        lax.all_gather(shards[7], "fsdp", axis=0, tiled=True),
        lax.all_gather(shards[8], "fsdp", axis=0, tiled=True),
        lax.all_gather(shards[9], "fsdp", axis=0, tiled=True),
        lax.all_gather(shards[10], "fsdp", axis=1, tiled=True),
        lax.all_gather(shards[11], "fsdp", axis=0, tiled=True),
    )


def scatter_whole(grads):
    return (
        lax.psum_scatter(grads[0], "fsdp", scatter_dimension=0, tiled=True),
        lax.psum_scatter(grads[1], "fsdp", scatter_dimension=0, tiled=True),
        lax.psum_scatter(grads[2], "fsdp", scatter_dimension=0, tiled=True),
        lax.psum_scatter(grads[3], "fsdp", scatter_dimension=0, tiled=True),
        lax.psum_scatter(grads[4], "fsdp", scatter_dimension=0, tiled=True),
        lax.psum_scatter(grads[5], "fsdp", scatter_dimension=0, tiled=True),
        lax.psum_scatter(grads[6], "fsdp", scatter_dimension=0, tiled=True),
        lax.psum_scatter(grads[7], "fsdp", scatter_dimension=0, tiled=True),
        lax.psum_scatter(grads[8], "fsdp", scatter_dimension=0, tiled=True),
        lax.psum_scatter(grads[9], "fsdp", scatter_dimension=0, tiled=True),
        lax.psum_scatter(grads[10], "fsdp", scatter_dimension=1, tiled=True),
        lax.psum_scatter(grads[11], "fsdp", scatter_dimension=0, tiled=True),
    )


def forward_pass(images, params, lookups):
    (
        gain_one,
        shift_one,
        qkv_weight,
        qv_bias,
        proj_weight,
        proj_bias,
        gain_two,
        shift_two,
        fc1_weight,
        fc1_bias,
        fc2_weight,
        fc2_bias,
    ) = params
    table_bias, allowed, partition, inverse = lookups
    image_count, tok_count, model_width = images.shape
    row_count = image_count * tok_count
    head_width = model_width // HEADS
    score_scale = head_width ** (-0.5)
    inputs_f = images.astype(jnp.float32).reshape(row_count, model_width)
    normed_one, unit_one, inv_one = normalize(
        inputs_f, gain_one.astype(jnp.float32), shift_one.astype(jnp.float32)
    )
    normed_one = normed_one.astype(jnp.bfloat16)
    qkv_shift = jnp.concatenate(
        [
            qv_bias[:model_width].astype(jnp.float32),
            jnp.zeros((model_width,), jnp.float32),
            qv_bias[model_width:].astype(jnp.float32),
        ]
    )
    qkv_rows = (
        jnp.dot(normed_one, qkv_weight, preferred_element_type=jnp.float32) + qkv_shift
    ).astype(jnp.bfloat16)
    qkv_win = to_windows(
        qkv_rows.reshape(image_count, tok_count, 3 * model_width), partition
    ).reshape(image_count, WIN_IMG, WINDOW, 3, HEADS, head_width)
    scores = window_scores(qkv_win[:, :, :, 0], qkv_win[:, :, :, 1], lookups, score_scale)
    row_top = jnp.max(scores, axis=-1, keepdims=True)
    log_total = row_top + jnp.log(jnp.sum(jnp.exp(scores - row_top), axis=-1, keepdims=True))
    soft_probs = jnp.exp(scores - log_total).astype(jnp.bfloat16)
    mixed = jnp.einsum(
        "bwhij,bwjhe->bwihe", soft_probs, qkv_win[:, :, :, 2], preferred_element_type=jnp.float32
    )
    attended = (
        from_windows(mixed.reshape(image_count, WIN_IMG, WINDOW, model_width), inverse)
        .astype(jnp.bfloat16)
        .reshape(row_count, model_width)
    )
    resid = (
        inputs_f
        + jnp.dot(attended, proj_weight, preferred_element_type=jnp.float32)
        + proj_bias.astype(jnp.float32)
    )
    normed_two, unit_two, inv_two = normalize(
        resid, gain_two.astype(jnp.float32), shift_two.astype(jnp.float32)
    )
    normed_two = normed_two.astype(jnp.bfloat16)
    pre_act = jnp.dot(normed_two, fc1_weight, preferred_element_type=jnp.float32) + fc1_bias.astype(
        jnp.float32
    )
    activ, gelu_slope = gelu_parts(pre_act)
    activ = activ.astype(jnp.bfloat16)
    output = (
        resid
        + jnp.dot(activ, fc2_weight, preferred_element_type=jnp.float32)
        + fc2_bias.astype(jnp.float32)
    ).astype(jnp.bfloat16)
    saved = (
        unit_one,
        inv_one,
        normed_one,
        qkv_win,
        log_total,
        attended,
        unit_two,
        inv_two,
        normed_two,
        gelu_slope,
        activ,
    )
    return (output.reshape(image_count, tok_count, model_width), saved)


def backward_pass(cotangent, saved, params, lookups):
    (
        gain_one,
        shift_one,
        qkv_weight,
        qv_bias,
        proj_weight,
        proj_bias,
        gain_two,
        shift_two,
        fc1_weight,
        fc1_bias,
        fc2_weight,
        fc2_bias,
    ) = params
    (
        unit_one,
        inv_one,
        normed_one,
        qkv_win,
        log_total,
        attended,
        unit_two,
        inv_two,
        normed_two,
        gelu_slope,
        activ,
    ) = saved
    table_bias, allowed, partition, inverse = lookups
    image_count, tok_count, model_width = cotangent.shape
    row_count = image_count * tok_count
    head_width = model_width // HEADS
    score_scale = head_width ** (-0.5)
    cot_rows = cotangent.reshape(row_count, model_width)
    cot_f = cot_rows.astype(jnp.float32)
    fc2_grad = jnp.dot(activ.T, cot_rows, preferred_element_type=jnp.float32)
    fc2_bias_grad = jnp.sum(cot_f, axis=0)
    grad_pre = jnp.dot(cot_rows, fc2_weight.T, preferred_element_type=jnp.float32) * gelu_slope
    grad_pre_b = grad_pre.astype(jnp.bfloat16)
    fc1_grad = jnp.dot(normed_two.T, grad_pre_b, preferred_element_type=jnp.float32)
    fc1_bias_grad = jnp.sum(grad_pre, axis=0)
    grad_normed = jnp.dot(grad_pre_b, fc1_weight.T, preferred_element_type=jnp.float32)
    grad_mid, gain_two_grad, shift_two_grad = norm_backward(
        grad_normed, unit_two, inv_two, gain_two.astype(jnp.float32)
    )
    grad_resid = cot_f + grad_mid
    grad_resid_b = grad_resid.astype(jnp.bfloat16)
    proj_grad = jnp.dot(attended.T, grad_resid_b, preferred_element_type=jnp.float32)
    proj_bias_grad = jnp.sum(grad_resid, axis=0)
    grad_att = jnp.dot(grad_resid_b, proj_weight.T, preferred_element_type=jnp.float32).astype(
        jnp.bfloat16
    )
    grad_mixed = to_windows(
        grad_att.reshape(image_count, tok_count, model_width), partition
    ).reshape(image_count, WIN_IMG, WINDOW, HEADS, head_width)
    queries = qkv_win[:, :, :, 0]
    key_rows = qkv_win[:, :, :, 1]
    value_rows = qkv_win[:, :, :, 2]
    scores = window_scores(queries, key_rows, lookups, score_scale)
    soft_full = jnp.exp(scores - log_total)
    soft_probs = soft_full.astype(jnp.bfloat16)
    value_grad = jnp.einsum(
        "bwhij,bwihe->bwjhe", soft_probs, grad_mixed, preferred_element_type=jnp.float32
    )
    prob_grad = jnp.einsum(
        "bwihe,bwjhe->bwhij", grad_mixed, value_rows, preferred_element_type=jnp.float32
    )
    score_grad = soft_full * (prob_grad - jnp.sum(soft_full * prob_grad, axis=-1, keepdims=True))
    pair_grad = jnp.sum(score_grad, axis=(0, 1))
    score_grad_b = score_grad.astype(jnp.bfloat16)
    query_grad = (
        jnp.einsum("bwhij,bwjhe->bwihe", score_grad_b, key_rows, preferred_element_type=jnp.float32)
        * score_scale
    )
    key_grad = (
        jnp.einsum("bwhij,bwihe->bwjhe", score_grad_b, queries, preferred_element_type=jnp.float32)
        * score_scale
    )
    stacked = jnp.stack([query_grad, key_grad, value_grad], axis=3).reshape(
        image_count, WIN_IMG, WINDOW, 3 * model_width
    )
    qkv_grad = from_windows(stacked, inverse).reshape(row_count, 3 * model_width)
    qkv_grad_b = qkv_grad.astype(jnp.bfloat16)
    qkv_grad_w = jnp.dot(normed_one.T, qkv_grad_b, preferred_element_type=jnp.float32)
    column_sums = jnp.sum(qkv_grad, axis=0)
    qv_grad = jnp.concatenate([column_sums[:model_width], column_sums[2 * model_width :]])
    grad_first = jnp.dot(qkv_grad_b, qkv_weight.T, preferred_element_type=jnp.float32)
    grad_low, gain_one_grad, shift_one_grad = norm_backward(
        grad_first, unit_one, inv_one, gain_one.astype(jnp.float32)
    )
    input_grad = (grad_resid + grad_low).reshape(image_count, tok_count, model_width)
    grads = (
        gain_one_grad,
        shift_one_grad,
        qkv_grad_w,
        qv_grad,
        proj_grad,
        proj_bias_grad,
        gain_two_grad,
        shift_two_grad,
        fc1_grad,
        fc1_bias_grad,
        fc2_grad,
        fc2_bias_grad,
    )
    return (input_grad, grads, pair_grad)


def per_device(
    block_input,
    out_cotangent,
    norm1_gain,
    norm1_bias,
    qkv_weight,
    qv_bias,
    proj_weight,
    proj_bias,
    norm2_gain,
    norm2_bias,
    fc1_weight,
    fc1_bias,
    fc2_weight,
    fc2_bias,
    bias_table,
    window_mask,
    rel_index,
    partition,
):
    shards = (
        norm1_gain,
        norm1_bias,
        qkv_weight,
        qv_bias,
        proj_weight,
        proj_bias,
        norm2_gain,
        norm2_bias,
        fc1_weight,
        fc1_bias,
        fc2_weight,
        fc2_bias,
    )
    pair_count = WINDOW * WINDOW
    table_rows = bias_table.shape[0]
    one_hot = (
        rel_index.reshape(pair_count, 1) == jnp.arange(table_rows, dtype=jnp.int32)[None, :]
    ).astype(jnp.float32)
    table_bias = jnp.transpose(
        jnp.dot(one_hot, bias_table.astype(jnp.float32), precision=lax.Precision.HIGHEST).reshape(
            WINDOW, WINDOW, HEADS
        ),
        (2, 0, 1),
    )
    allowed = (window_mask == 1)[None, :, None, :, :]
    tok_count = partition.shape[0]
    inverse = (
        jnp.zeros((tok_count,), jnp.int32).at[partition].set(jnp.arange(tok_count, dtype=jnp.int32))
    )
    lookups = (table_bias, allowed, partition, inverse)
    held_params = fetch_pass_fwd(shards)
    micro_index = 0
    output, saved = forward_pass(block_input, held_params, lookups)
    kept = [saved]
    held_params = fetch_pass_bwd(shards)
    input_grads = [None] * MICRO
    pair_total = jnp.zeros((HEADS, WINDOW, WINDOW), jnp.float32)
    grad_totals = None
    for micro_index in reversed(range(MICRO)):
        input_grad, grads, pair_grad = backward_pass(
            out_cotangent, kept[micro_index], held_params, lookups
        )
        input_grads[micro_index] = input_grad
        pair_total = pair_grad
        grad_totals = grads
    grad_totals = scatter_whole(grad_totals)
    table_local = jnp.dot(
        one_hot.T,
        jnp.transpose(pair_total, (1, 2, 0)).reshape(pair_count, HEADS),
        precision=lax.Precision.HIGHEST,
    )
    table_grad = lax.psum(table_local, "fsdp")
    input_grad_all = input_grads[0]
    return (
        output,
        input_grad_all,
        grad_totals[0],
        grad_totals[1],
        grad_totals[2],
        grad_totals[3],
        grad_totals[4],
        grad_totals[5],
        grad_totals[6],
        grad_totals[7],
        grad_totals[8],
        grad_totals[9],
        grad_totals[10],
        grad_totals[11],
        table_grad,
    )


def solution(mesh):
    placed = (
        P("fsdp", None, None),
        P("fsdp", None, None),
        P("fsdp"),
        P("fsdp"),
        P("fsdp", None),
        P("fsdp"),
        P("fsdp", None),
        P("fsdp"),
        P("fsdp"),
        P("fsdp"),
        P("fsdp", None),
        P("fsdp"),
        P(None, "fsdp"),
        P("fsdp"),
        P(),
        P(),
        P(),
        P(),
    )
    return jax.shard_map(
        per_device,
        mesh=mesh,
        in_specs=placed,
        out_specs=(
            P("fsdp", None, None),
            P("fsdp", None, None),
            P("fsdp"),
            P("fsdp"),
            P("fsdp", None),
            P("fsdp"),
            P("fsdp", None),
            P("fsdp"),
            P("fsdp"),
            P("fsdp"),
            P("fsdp", None),
            P("fsdp"),
            P(None, "fsdp"),
            P("fsdp"),
            P(),
        ),
        check_vma=False,
    )
```

profile of v0, /device:TPU:0, one launch (start us, length us, event | category | flops | bytes accessed | tf_op | source)
XLA Modules:
  0.0 726.6 jit_solution(5990578621208779468)
XLA Ops:
  18.9 42.4 %all-reduce.17 = (bf16[512]{0:T(512)(128)(2,1)S(1)}, bf16[1024]{0:T(1024)(128)(2,1)S(1)}, bf16[512]{0:T(512)(128)(2,1)S(1)}, bf16[512]{0:T(512)(128)(2,1)S(1)}, ...) all-reduce(bf16[512]{0:T(512)(128)(2,1)S(1)} %dynamic-update-slice., ...), channel_id=1, replica_groups=mesh['fsdp'=32] {'fsdp'}, use_global_device_ids=true, to_apply=%add.3 | all-reduce | flops 6144 | bytes 24576
  66.3 45.4 %all_gather.46 = bf16[512,512]{1,0:T(8,128)(2,1)} all-gather(bf16[16,512]{1,0:T(8,128)(2,1)S(1)} %copy-done.15), channel_id=1, replica_groups=mesh['fsdp'=32] {'fsdp'}, dimensions={0}, use_global_device_ids=true | all-gather | bytes 540672 | tf_op jit(solution)/shard_map/all_gather | solution.py:67
  111.7 2.0 fusion
  116.3 3.0 copy.58
  124.3 1.9 reshape.401
  128.0 3.6 multiply_convert_fusion
  131.5 53.5 %all-gather.8.cloned.1.call-done = bf16[2048,512]{0,1:T(8,128)(2,1)} async-done(((bf16[2048,16]{0,1:T(8,128)(2,1)}), bf16[2048,512]{0,1:T(8,128)(2,1)}) %all-gather.8.cloned.1.call-update) | async-done | bytes 2097168 | tf_op jit(solution)/shard_map/all_gather | solution.py:73
  185.0 3.9 fusion.82
  198.7 2.1 gather.31
  202.0 1.8 multiply_reduce_fusion
  206.9 2.0 pad_maximum_fusion
  208.9 5.8 copy.81
  214.7 4.0 reshape.402
  218.7 2.1 gather_fusion.3
  220.8 3.8 fusion.19
  225.8 2.8 fusion.50
  229.5 2.7 fusion.59
  235.5 2.3 fusion.44
  240.4 39.1 %all-reduce.16 = (f32[512]{0:T(512)S(1)}, f32[512]{0:T(512)S(1)}, f32[1024]{0:T(1024)S(1)}, f32[512]{0:T(512)S(1)}, f32[512]{0:T(512)S(1)}, /*index=5*/f32[512]{...) all-reduce(f32[512]{0:T(512)S(1)} %get-tuple-element.62, ...), channel_id=2, replica_groups=mesh['fsdp'=32] {'fsdp'}, use_global_device_ids=true, to_apply=%region_13.14.clone | all-reduce | flops 8848 | bytes 70784
  284.2 3.2 fusion.16
  287.4 41.7 %reduce-scatter.7.cloned.1.call-done = f32[16,512]{1,0:T(8,128)} async-done(((f32[512,512]{1,0:T(8,128)}), f32[16,512]{1,0:T(8,128)}) %reduce-scatter.7.cloned.1.call-update) | async-done | bytes 32784 | tf_op jit(solution)/shard_map/reduce_scatter | solution.py:101
  329.1 104.1 %reduce-scatter.5.cloned.1.call-done = f32[16,1536]{1,0:T(8,128)} async-done(((f32[512,1536]{1,0:T(8,128)}), f32[16,1536]{1,0:T(8,128)}) %reduce-scatter.5.cloned.1.call-update) | async-done | bytes 98320 | tf_op jit(solution)/shard_map/reduce_scatter | solution.py:99
  433.2 144.7 %reduce-scatter.9.cloned.1.call-done = f32[16,2048]{1,0:T(8,128)} async-done(((f32[512,2048]{1,0:T(8,128)}), f32[16,2048]{1,0:T(8,128)}) %reduce-scatter.9.cloned.1.call-update) | async-done | bytes 131088 | tf_op jit(solution)/shard_map/reduce_scatter | solution.py:105
  577.9 141.9 %reduce-scatter.11.cloned.1.call-done = f32[2048,16]{0,1:T(8,128)} async-done(((f32[2048,512]{0,1:T(8,128)}), f32[2048,16]{0,1:T(8,128)}) %reduce-scatter.11.cloned.1.call-update) | async-done | bytes 131088 | tf_op jit(solution)/shard_map/reduce_scatter | solution.py:107
  (170 shorter events, 52.0 us)
Async XLA Ops:
  7.2 56.0 %copy-start = (bf16[169,16]{0,1:T(8,128)(2,1)S(1)}, bf16[169,16]{0,1:T(8,128)(2,1)}, u32[]{:S(2)}) copy-start(bf16[169,16]{0,1:T(8,128)(2,1)} %param.32) | copy-start | bytes 16228
  7.2 58.7 %copy-start.6 = (bf16[1,196,512]{2,1,0:T(8,128)(2,1)S(1)}, bf16[1,196,512]{2,1,0:T(8,128)(2,1)}, u32[]{:S(2)}) copy-start(bf16[1,196,512]{2,1,0:T(8,128)(2,1)} %param.18) | copy-start | bytes 602116
  7.2 59.1 %copy-start.15 = (bf16[16,512]{1,0:T(8,128)(2,1)S(1)}, bf16[16,512]{1,0:T(8,128)(2,1)}, u32[]{:S(2)}) copy-start(bf16[16,512]{1,0:T(8,128)(2,1)} %param.24) | copy-start | bytes 49156
  7.2 104.5 %all-gather.4.cloned.1.call-start = ((), (), s32[]{:S(2)}) async-start(), calls=%async_computation.4 | async-start | bytes 1622016 | tf_op jit(solution)/shard_map/all_gather | solution.py:65
  7.9 120.0 %all-gather.6.cloned.1.call-start = ((), (), s32[]{:S(2)}) async-start(), calls=%async_computation.5 | async-start | bytes 2162688 | tf_op jit(solution)/shard_map/all_gather | solution.py:71
  8.7 176.3 %all-gather.8.cloned.1.call-start = ((), (), s32[]{:S(2)}) async-start(), calls=%async_computation.6 | async-start | bytes 2162688 | tf_op jit(solution)/shard_map/all_gather | solution.py:73
  9.4 319.7 %reduce-scatter.7.cloned.1.call-start = ((), (), s32[]{:S(2)}) async-start(), calls=%async_computation.8 | async-start | bytes 1081344 | tf_op jit(solution)/shard_map/reduce_scatter | solution.py:101
  63.8 55.6 %copy-start.30 = (pred[4,49]{1,0:T(4,128)(4,1)}, pred[4,49]{1,0:T(4,128)(4,1)S(1)}, u32[]{:S(2)}) copy-start(pred[4,49]{1,0:T(4,128)(4,1)S(1)} %broadcast_in_dim.97) | copy-start | bytes 592
  64.4 49.2 %copy-start.20 = (f32[512]{0:T(512)}, f32[512]{0:T(512)S(1)}, u32[]{:S(2)}) copy-start(f32[512]{0:T(512)S(1)} %convert_element_type.103) | copy-start | bytes 6148
  66.2 61.0 %copy-start.22 = (pred[196]{0:T(512)(128)(4,1)}, pred[196]{0:T(512)(128)(4,1)S(1)}, u32[]{:S(2)}) copy-start(pred[196]{0:T(512)(128)(4,1)S(1)} %compare_and_fusion.1) | copy-start | bytes 592
  66.3 48.5 %copy-start.18 = (f32[196]{0:T(256)}, f32[196]{0:T(256)S(1)}, u32[]{:S(2)}) copy-start(f32[196]{0:T(256)S(1)} %add_rsqrt_fusion.1) | copy-start | bytes 2356
  124.3 3.0 copy-start.7
  124.3 3.0 copy-start.26
  185.0 3.9 copy-start.8
  188.9 3.1 copy-start.23
  193.5 239.7 %reduce-scatter.5.cloned.1.call-start = ((), (), s32[]{:S(2)}) async-start(), calls=%async_computation.7 | async-start | bytes 3244032 | tf_op jit(solution)/shard_map/reduce_scatter | solution.py:99
  195.2 5.5 copy-start.31
  224.6 353.2 %reduce-scatter.9.cloned.1.call-start = ((), (), s32[]{:S(2)}) async-start(), calls=%async_computation.9 | async-start | bytes 4325376 | tf_op jit(solution)/shard_map/reduce_scatter | solution.py:105
  228.6 491.2 %reduce-scatter.11.cloned.1.call-start = ((), (), s32[]{:S(2)}) async-start(), calls=%async_computation.10 | async-start | bytes 4325376 | tf_op jit(solution)/shard_map/reduce_scatter | solution.py:107
  232.2 3.2 copy-start.1
  238.0 2.3 copy-start.24
  238.0 2.3 copy-start.25
  238.1 2.3 copy-start.27
  238.1 2.3 copy-start.28
  (16 other events, 24.6 us)
Sparse Core Ops, SparseCore 0:
  10.9 57.9 all-gather.3
  71.7 55.2 all-gather.5
  130.0 55.0 all-gather.7
  193.6 135.4 reduce-scatter.6
  334.9 98.2 reduce-scatter.4
  435.9 141.9 reduce-scatter.8
  580.7 139.0 reduce-scatter.10
where the time goes:
time: 728 us; the launch traced here: 727 us
  waiting for transfers between devices  488 us (67%)
  blocking collectives  127 us (17%)
  local copies, waits for them, and re-layouts  49.8 us (7%)
  matrix products  35.1 us (5%)
  between operations  14.7 us (2%)
  other arithmetic  11.5 us (2%)
    reduce_scatter x1, waiting for transfers between devices, scatter_whole(): lax.psum_scatter(grads[8], 'fsdp', scatter_dimension=0, tiled=True)  145 us
    reduce_scatter x1, waiting for transfers between devices, scatter_whole(): lax.psum_scatter(grads[10], 'fsdp', scatter_dimension=1, tiled=True)  142 us
    reduce_scatter x1, waiting for transfers between devices, scatter_whole(): lax.psum_scatter(grads[2], 'fsdp', scatter_dimension=0, tiled=True)  104 us
    unnamed x2, blocking collectives  81.5 us
    all_gather x1, waiting for transfers between devices, fetch_pass_fwd(): lax.all_gather(shards[10], 'fsdp', axis=1, tiled=True)  53.5 us
    all_gather x1, blocking collectives, fetch_pass_fwd(): lax.all_gather(shards[4], 'fsdp', axis=0, tiled=True)  45.4 us
    reduce_scatter x1, waiting for transfers between devices, scatter_whole(): lax.psum_scatter(grads[4], 'fsdp', scatter_dimension=0, tiled=True)  41.7 us
    unnamed x91, local copies, waits for them, and re-layouts  16.4 us
  transfers between devices with their start and end apart: 7, of which 5 were waited for; matrix products, arithmetic and copies ran while one was open for 12% of the time, Pallas kernels for 0%

commit v1 on v0

--- a/solution.py
+++ b/solution.py
@@ -1,6 +1,10 @@
+import functools
+
 import jax
 import jax.numpy as jnp
 from jax import lax
+from jax.experimental import pallas as pl
+from jax.experimental.pallas import tpu as pltpu
 from jax.sharding import PartitionSpec as P
 
 HEADS = 16
@@ -58,54 +62,333 @@
     return jnp.where(allowed, raw, NEG_FILL)
 
 
-def fetch_pass_fwd(shards):
+MESH = pl.DeviceIdType.MESH
+
+
+def bit_orders(bit_count):
+    rest = list(range(1, bit_count))
+    return ([0] + rest, [0] + rest[1:] + rest[:1])
+
+
+def part_order(part, bit_count):
+    return bit_orders(bit_count)[part % 2]
+
+
+def place(bit_count):
+    me = lax.axis_index("fsdp")
+    mine = [lax.rem(lax.div(me, 1 << b), 2) for b in range(bit_count)]
+    partner = [me + (1 - 2 * mine[b]) * (1 << b) for b in range(bit_count)]
+    return (mine, partner)
+
+
+def greet(partner):
+    barrier = pltpu.get_barrier_semaphore()
+    for other in partner:
+        pl.semaphore_signal(barrier, inc=1, device_id=(other,), device_id_type=MESH)
+    pl.semaphore_wait(barrier, len(partner))
+
+
+def gather_kernel(bit_count, part_count, *refs):
+    ins, outs = refs[:part_count], refs[part_count : 2 * part_count]
+    send_sem, recv_sem, local_sem = refs[2 * part_count :]
+    mine, partner = place(bit_count)
+    locals_ = []
+    whole_index = tuple(mine[b] for b in reversed(range(bit_count)))
+    for p in range(part_count):
+        copy = pltpu.make_async_copy(ins[p], outs[p].at[whole_index], local_sem.at[p])
+        copy.start()
+        locals_.append(copy)
+    greet(partner)
+    pending = [None] * part_count
+    sent = []
+    done = [[] for _ in range(part_count)]
+    for step in range(bit_count):
+        for p in range(part_count):
+            bit = part_order(p, bit_count)[bit_count - 1 - step]
+            if step == 1:
+                locals_[p].wait()
+            if pending[p] is not None:
+                pending[p].wait_recv()
+            index = tuple(
+                slice(None) if b in done[p] else mine[b] for b in reversed(range(bit_count))
+            )
+            view = outs[p].at[index]
+            copy = pltpu.make_async_remote_copy(
+                src_ref=ins[p] if step == 0 else view,
+                dst_ref=view,
+                send_sem=send_sem.at[p, step],
+                recv_sem=recv_sem.at[p, step],
+                device_id=(partner[bit],),
+                device_id_type=MESH,
+            )
+            copy.start()
+            pending[p] = copy
+            sent.append(copy)
+            done[p].append(bit)
+    for p in range(part_count):
+        pending[p].wait_recv()
+    for copy in sent:
+        copy.wait_send()
+
+
+def gather_parts(parts, count):
+    bit_count = count.bit_length() - 1
+    part_count = len(parts)
+    spec = pl.BlockSpec(memory_space=pltpu.VMEM)
+    outs = pl.pallas_call(
+        functools.partial(gather_kernel, bit_count, part_count),
+        out_shape=[
+            jax.ShapeDtypeStruct((2,) * bit_count + part.shape, part.dtype) for part in parts
+        ],
+        in_specs=[spec] * part_count,
+        out_specs=[spec] * part_count,
+        scratch_shapes=[
+            pltpu.SemaphoreType.DMA((part_count, bit_count)),
+            pltpu.SemaphoreType.DMA((part_count, bit_count)),
+            pltpu.SemaphoreType.DMA((part_count,)),
+        ],
+        compiler_params=pltpu.CompilerParams(collective_id=0, has_side_effects=True),
+        name="gather_parts",
+    )(*parts)
+    return [out.reshape((count,) + part.shape) for out, part in zip(outs, parts)]
+
+
+def scatter_kernel(bit_count, part_count, *refs):
+    count = 1 << bit_count
+    ins, table_in = refs[:part_count], refs[part_count]
+    outs, table_out = refs[part_count + 1 : 2 * part_count + 1], refs[2 * part_count + 1]
+    rest = list(refs[2 * part_count + 2 :])
+    send_sem, recv_sem, table_send, table_recv = rest[:4]
+    table_got, table_sum = rest[4:6]
+    got = rest[6 : 6 + part_count * bit_count]
+    held = rest[6 + part_count * bit_count :]
+    mine, partner = place(bit_count)
+    greet(partner)
+    sent = []
+
+    def table_start(step):
+        copy = pltpu.make_async_remote_copy(
+            src_ref=table_in if step == 0 else table_sum.at[step - 1],
+            dst_ref=table_got.at[step],
+            send_sem=table_send.at[step],
+            recv_sem=table_recv.at[step],
+            device_id=(partner[step],),
+            device_id_type=MESH,
+        )
+        copy.start()
+        sent.append(copy)
+        return copy
+
+    def start(p, step):
+        bit = part_order(p, bit_count)[step]
+        source = ins[p] if step == 0 else held[p * (bit_count - 1) + step - 1]
+        copy = pltpu.make_async_remote_copy(
+            src_ref=source.at[:, 1 - mine[bit]],
+            dst_ref=got[p * bit_count + step],
+            send_sem=send_sem.at[p, step],
+            recv_sem=recv_sem.at[p, step],
+            device_id=(partner[bit],),
+            device_id_type=MESH,
+        )
+        copy.start()
+        sent.append(copy)
+        return copy
+
+    def add(p, step):
+        bit = part_order(p, bit_count)[step]
+        source = ins[p] if step == 0 else held[p * (bit_count - 1) + step - 1]
+        arrived = got[p * bit_count + step]
+        high, low = arrived.shape[0], arrived.shape[1]
+
+        def total(k):
+            i, j = k // low, k % low
+            return source[i, mine[bit], j].astype(jnp.float32) + arrived[i, j].astype(jnp.float32)
+
+        if step == bit_count - 1:
+            outs[p][...] = total(0)
+            return
+        target = held[p * (bit_count - 1) + step]
+        low_next = target.shape[2]
+
+        def body(k, carry):
+            target[k // (2 * low_next), (k // low_next) % 2, k % low_next] = total(k).astype(
+                target.dtype
+            )
+            return carry
+
+        lax.fori_loop(0, high * low, body, 0)
+
+    pending = [start(p, 0) for p in range(part_count)]
+    table_pending = table_start(0)
+    for step in range(bit_count):
+        for p in range(part_count):
+            pending[p].wait_recv()
+            add(p, step)
+            if step + 1 < bit_count:
+                pending[p] = start(p, step + 1)
+        table_pending.wait_recv()
+        total_table = (table_in[...] if step == 0 else table_sum[step - 1]) + table_got[step]
+        if step + 1 < bit_count:
+            table_sum[step] = total_table
+            table_pending = table_start(step + 1)
+        else:
+            table_out[...] = total_table
+    for copy in sent:
+        copy.wait_send()
+
+
+def remaining_shape(order, step):
+    left = sorted(order[step:])
+    place_of = left.index(order[step])
+    return (1 << (len(left) - 1 - place_of), 2, 1 << place_of)
+
+
+def scatter_parts(parts, table, count):
+    bit_count = count.bit_length() - 1
+    part_count = len(parts)
+    spec = pl.BlockSpec(memory_space=pltpu.VMEM)
+    got, held, shaped = [], [], []
+    for p, part in enumerate(parts):
+        order = part_order(p, bit_count)
+        block = part.shape[1:]
+        for step in range(bit_count):
+            high, two, low = remaining_shape(order, step)
+            got.append(pltpu.VMEM((high, low) + block, part.dtype))
+            if step == 0:
+                shaped.append(part.reshape((high, two, low) + block))
+            else:
+                held.append(pltpu.VMEM((high, two, low) + block, part.dtype))
+    outs = pl.pallas_call(
+        functools.partial(scatter_kernel, bit_count, part_count),
+        out_shape=[jax.ShapeDtypeStruct(part.shape[1:], jnp.float32) for part in parts]
+        + [jax.ShapeDtypeStruct(table.shape, jnp.float32)],
+        in_specs=[spec] * (part_count + 1),
+        out_specs=[spec] * (part_count + 1),
+        scratch_shapes=[
+            pltpu.SemaphoreType.DMA((part_count, bit_count)),
+            pltpu.SemaphoreType.DMA((part_count, bit_count)),
+            pltpu.SemaphoreType.DMA((bit_count,)),
+            pltpu.SemaphoreType.DMA((bit_count,)),
+            pltpu.VMEM((bit_count,) + table.shape, jnp.float32),
+            pltpu.VMEM((bit_count,) + table.shape, jnp.float32),
+        ]
+        + got
+        + held,
+        compiler_params=pltpu.CompilerParams(collective_id=1, has_side_effects=True),
+        name="scatter_parts",
+    )(*shaped, table)
+    return (outs[:part_count], outs[part_count])
+
+
+LANES = 128
+ROWS = 16
+
+
+def fold(block):
+    r, c = block.shape[-2:]
+    rows = max(r, ROWS)
+    return block.reshape(block.shape[:-2] + (rows, r * c // rows))
+
+
+def unfold(blocks, r, c):
+    return blocks[..., : r * c // blocks.shape[-2]].reshape(blocks.shape[:-2] + (r, c))
+
+
+def with_vectors(block, flat):
+    rows, width = block.shape[-2:]
+    extra = -(-flat.shape[-1] // rows)
+    total = -(-(width + extra) // LANES) * LANES - width
+    padded = jnp.pad(flat, [(0, 0)] * (flat.ndim - 1) + [(0, rows * total - flat.shape[-1])])
+    return jnp.concatenate([block, padded.reshape(flat.shape[:-1] + (rows, total))], axis=-1)
+
+
+def fetch_all(shards):
+    count = lax.axis_size("fsdp")
+    vectors = [shards[k] for k in (0, 1, 3, 5, 6, 7, 9, 11)]
+    lengths = [v.shape[0] for v in vectors]
+    qkv, proj, fc1, fc2_t = shards[2], shards[4], shards[8], shards[10].T
+    folded_proj = fold(proj)
+    parts = [
+        fold(fc1),
+        fold(fc2_t),
+        fold(qkv),
+        with_vectors(folded_proj, jnp.concatenate(vectors)),
+    ]
+    fc1_all, fc2_all, qkv_all, proj_all = gather_parts(parts, count)
+
+    def whole(blocks, shard):
+        r, c = shard.shape
+        return unfold(blocks, r, c).reshape(count * r, c)
+
+    flat = proj_all[:, :, folded_proj.shape[1] :].reshape(count, -1)
+    start, gathered = 0, []
+    for length in lengths:
+        gathered.append(flat[:, start : start + length].reshape(-1))
+        start += length
     return (
-        lax.all_gather(shards[0], "fsdp", axis=0, tiled=True),
-        lax.all_gather(shards[1], "fsdp", axis=0, tiled=True),
-        lax.all_gather(shards[2], "fsdp", axis=0, tiled=True),
-        lax.all_gather(shards[3], "fsdp", axis=0, tiled=True),
-        lax.all_gather(shards[4], "fsdp", axis=0, tiled=True),
-        lax.all_gather(shards[5], "fsdp", axis=0, tiled=True),
-        lax.all_gather(shards[6], "fsdp", axis=0, tiled=True),
-        lax.all_gather(shards[7], "fsdp", axis=0, tiled=True),
-        lax.all_gather(shards[8], "fsdp", axis=0, tiled=True),
-        lax.all_gather(shards[9], "fsdp", axis=0, tiled=True),
-        lax.all_gather(shards[10], "fsdp", axis=1, tiled=True),
-        lax.all_gather(shards[11], "fsdp", axis=0, tiled=True),
-    )
-
-
-def fetch_pass_bwd(shards):
+        gathered[0],
+        gathered[1],
+        whole(qkv_all, qkv),
+        gathered[2],
+        whole(proj_all, proj),
+        gathered[3],
+        gathered[4],
+        gathered[5],
+        whole(fc1_all, fc1),
+        gathered[6],
+        whole(fc2_all, fc2_t),
+        gathered[7],
+    )
+
+
+def scatter_whole(grads, table_local):
+    count = lax.axis_size("fsdp")
+
+    def blocks(grad):
+        return fold(grad.astype(jnp.bfloat16).reshape(count, grad.shape[0] // count, grad.shape[1]))
+
+    vectors = [
+        grads[k].astype(jnp.bfloat16).reshape(count, -1) for k in (0, 1, 3, 5, 6, 7, 9, 11)
+    ]
+    folded_proj = blocks(grads[4])
+    parts = [
+        blocks(grads[10]),
+        blocks(grads[8]),
+        blocks(grads[2]),
+        with_vectors(folded_proj, jnp.concatenate(vectors, axis=1)),
+    ]
+    entries = table_local.size
+    table_rows = -(-entries // (8 * LANES)) * 8
+    table_pad = jnp.pad(table_local.reshape(-1), (0, table_rows * LANES - entries)).reshape(
+        table_rows, LANES
+    )
+    (fc2_b, fc1_b, qkv_b, proj_b), table_sum = scatter_parts(parts, table_pad, count)
+
+    def own(block, grad):
+        return unfold(block, grad.shape[0] // count, grad.shape[1])
+
+    flat = proj_b[:, folded_proj.shape[2] :].reshape(-1)
+    start, pieces = 0, []
+    for vector in vectors:
+        pieces.append(flat[start : start + vector.shape[1]])
+        start += vector.shape[1]
+    table_grad = table_sum.reshape(-1)[:entries].reshape(table_local.shape)
     return (
-        lax.all_gather(shards[0], "fsdp", axis=0, tiled=True),
-        lax.all_gather(shards[1], "fsdp", axis=0, tiled=True),
-        lax.all_gather(shards[2], "fsdp", axis=0, tiled=True),
-        lax.all_gather(shards[3], "fsdp", axis=0, tiled=True),
-        lax.all_gather(shards[4], "fsdp", axis=0, tiled=True),
-        lax.all_gather(shards[5], "fsdp", axis=0, tiled=True),
-        lax.all_gather(shards[6], "fsdp", axis=0, tiled=True),
-        lax.all_gather(shards[7], "fsdp", axis=0, tiled=True),
-        lax.all_gather(shards[8], "fsdp", axis=0, tiled=True),
-        lax.all_gather(shards[9], "fsdp", axis=0, tiled=True),
-        lax.all_gather(shards[10], "fsdp", axis=1, tiled=True),
-        lax.all_gather(shards[11], "fsdp", axis=0, tiled=True),
-    )
-
-
-def scatter_whole(grads):
-    return (
-        lax.psum_scatter(grads[0], "fsdp", scatter_dimension=0, tiled=True),
-        lax.psum_scatter(grads[1], "fsdp", scatter_dimension=0, tiled=True),
-        lax.psum_scatter(grads[2], "fsdp", scatter_dimension=0, tiled=True),
-        lax.psum_scatter(grads[3], "fsdp", scatter_dimension=0, tiled=True),
-        lax.psum_scatter(grads[4], "fsdp", scatter_dimension=0, tiled=True),
-        lax.psum_scatter(grads[5], "fsdp", scatter_dimension=0, tiled=True),
-        lax.psum_scatter(grads[6], "fsdp", scatter_dimension=0, tiled=True),
-        lax.psum_scatter(grads[7], "fsdp", scatter_dimension=0, tiled=True),
-        lax.psum_scatter(grads[8], "fsdp", scatter_dimension=0, tiled=True),
-        lax.psum_scatter(grads[9], "fsdp", scatter_dimension=0, tiled=True),
-        lax.psum_scatter(grads[10], "fsdp", scatter_dimension=1, tiled=True),
-        lax.psum_scatter(grads[11], "fsdp", scatter_dimension=0, tiled=True),
+        (
+            pieces[0],
+            pieces[1],
+            own(qkv_b, grads[2]),
+            pieces[2],
+            own(proj_b, grads[4]),
+            pieces[3],
+            pieces[4],
+            pieces[5],
+            own(fc1_b, grads[8]),
+            pieces[6],
+            own(fc2_b, grads[10]).T,
+            pieces[7],
+        ),
+        table_grad,
     )
 
 
@@ -175,7 +458,7 @@
     activ = activ.astype(jnp.bfloat16)
     output = (
         resid
-        + jnp.dot(activ, fc2_weight, preferred_element_type=jnp.float32)
+        + jnp.dot(activ, fc2_weight.T, preferred_element_type=jnp.float32)
         + fc2_bias.astype(jnp.float32)
     ).astype(jnp.bfloat16)
     saved = (
@@ -229,9 +512,9 @@
     score_scale = head_width ** (-0.5)
     cot_rows = cotangent.reshape(row_count, model_width)
     cot_f = cot_rows.astype(jnp.float32)
-    fc2_grad = jnp.dot(activ.T, cot_rows, preferred_element_type=jnp.float32)
+    fc2_grad = jnp.dot(cot_rows.T, activ, preferred_element_type=jnp.float32)
     fc2_bias_grad = jnp.sum(cot_f, axis=0)
-    grad_pre = jnp.dot(cot_rows, fc2_weight.T, preferred_element_type=jnp.float32) * gelu_slope
+    grad_pre = jnp.dot(cot_rows, fc2_weight, preferred_element_type=jnp.float32) * gelu_slope
     grad_pre_b = grad_pre.astype(jnp.bfloat16)
     fc1_grad = jnp.dot(normed_two.T, grad_pre_b, preferred_element_type=jnp.float32)
     fc1_bias_grad = jnp.sum(grad_pre, axis=0)
@@ -353,11 +636,10 @@
         jnp.zeros((tok_count,), jnp.int32).at[partition].set(jnp.arange(tok_count, dtype=jnp.int32))
     )
     lookups = (table_bias, allowed, partition, inverse)
-    held_params = fetch_pass_fwd(shards)
+    held_params = fetch_all(shards)
     micro_index = 0
     output, saved = forward_pass(block_input, held_params, lookups)
     kept = [saved]
-    held_params = fetch_pass_bwd(shards)
     input_grads = [None] * MICRO
     pair_total = jnp.zeros((HEADS, WINDOW, WINDOW), jnp.float32)
     grad_totals = None
@@ -368,13 +650,12 @@
         input_grads[micro_index] = input_grad
         pair_total = pair_grad
         grad_totals = grads
-    grad_totals = scatter_whole(grad_totals)
     table_local = jnp.dot(
         one_hot.T,
         jnp.transpose(pair_total, (1, 2, 0)).reshape(pair_count, HEADS),
         precision=lax.Precision.HIGHEST,
     )
-    table_grad = lax.psum(table_local, "fsdp")
+    grad_totals, table_grad = scatter_whole(grad_totals, table_local)
     input_grad_all = input_grads[0]
     return (
         output,

time: 728 us -> 195 us (0.27)
  waiting for transfers between devices: 488 us -> 0 us
  blocking collectives: 127 us -> 0 us
  Pallas kernels: 0 us -> 99.5 us
  between operations: 14.7 us -> 1.38 us
    reduce_scatter x4 -> x0, waiting for transfers between devices: 432 us -> none  [the longest x1 145 us: scatter_whole(): lax.psum_scatter(grads[8], 'fsdp', scatter_dimension=0, tiled=True)]
    pallas_call x0 -> x2, Pallas kernels: none -> 99.5 us  [the longest x1 51.4 us: gather_parts(): pl.pallas_call(functools.partial(gather_kernel, bit_count, part_count), o...]
    unnamed x2 -> x0, blocking collectives: 81.5 us -> none
    all_gather x3 -> x0, waiting for transfers between devices: 53.5 us -> none  [the longest x1 53.5 us: fetch_pass_fwd(): lax.all_gather(shards[10], 'fsdp', axis=1, tiled=True)]
    all_gather x1 -> x0, blocking collectives: 45.4 us -> none  [fetch_pass_fwd(): lax.all_gather(shards[4], 'fsdp', axis=0, tiled=True)]
    unnamed x91 -> x84, local copies, waits for them, and re-layouts: 16.4 us -> 8.88 us
  transfers between devices with their start and end apart: 7 -> 0, of which waited for: 5 -> 0; matrix products, arithmetic and copies ran while one was open for 12% -> 0% of each run, Pallas kernels for 0% -> 0%
where the time goes in v1:
time: 195 us; the launch traced here: 194 us
  Pallas kernels  99.5 us (51%)
  local copies, waits for them, and re-layouts  52.1 us (27%)
  matrix products  29.8 us (15%)
  other arithmetic  11.4 us (6%)
    pallas_call x1, Pallas kernels, gather_parts(): pl.pallas_call(functools.partial(gather_kernel, bit_count, part_count), o...  51.4 us
    pallas_call x1, Pallas kernels, scatter_parts(): pl.pallas_call(functools.partial(scatter_kernel, bit_count, part_count),...  48.1 us
    another operation x4, local copies, waits for them, and re-layouts, from_windows(): window_rows.reshape(window_rows.shape[0], inverse.shape[0], window_rows.s...  13.2 us
    gather x6, local copies, waits for them, and re-layouts, to_windows(): picked = jnp.take(token_rows, partition, axis=1)  9.64 us
    unnamed x84, local copies, waits for them, and re-layouts  8.88 us
    concatenate x1, local copies, waits for them, and re-layouts, fetch_all(): jnp.concatenate(vectors)  5.47 us

profile of v1, /device:TPU:0, one launch (start us, length us, event | category | flops | bytes accessed | tf_op | source)
XLA Modules:
  0.0 194.2 jit_solution(4345419273268508322)
XLA Ops:
  0.7 5.5 %concatenate.29 = bf16[192]{0:T(256)(128)(2,1)S(1)} concatenate(bf16[16]{0:T(256)(128)(2,1)} %param.20, bf16[16]{0:T(256)(128)(2,1)} %param.21, bf16[32]{0:T(256)(128)(2,1)} %param.23, bf16[16]{0:T(256)(128)(2,1)} %param.25, bf16[16]{0:T(256)(128)(2,1)} %param.26, bf16[16]{0:T(256)(128)(2,1)} %param.27, bf16[64]{0:T(256)(128)(2,1)} %param.29, bf16[16]{0:T(256)(128)(2,1)} %param.31), dimensions={0} | concatenate | bytes 768 | tf_op jit(solution)/shard_map/concatenate | solution.py:315
  7.5 51.4 %gather_parts.1 = (bf16[2,2,2,2,2,16,2048]{6,5,4,3,2,1,0:T(8,128)(2,1)}, bf16[2,2,2,2,2,16,2048]{6,5,4,3,2,1,0:T(8,128)(2,1)}, bf16[2,2,2,2,2,16,1536]{6,5,4,3,2...) custom-call(bf16[16,2048]{1,0:T(8,128)(2,1)} %refs_0_.1, bf16[16,2048]{1,0:T(8,128)(2,1)} %bitcast.196, ...), custom_call_target="tpu_custom_call" | custom-call | tf_op jit(solution)/shard_map/gather_parts/pallas_call | solution.py:138
  62.7 1.9 gather_fusion
  64.6 3.0 %reshape.602 = bf16[1,4,49,3,16,32]{5,4,3,2,1,0:T(8,128)(2,1)S(1)} reshape(bf16[196,1536]{1,0:T(8,128)(2,1)} %gather_fusion) | data formatting | bytes 1204224 | tf_op jit(solution)/shard_map/jit(_take)/gather | solution.py:46
  67.6 3.1 %copy.61 = bf16[1,4,49,3,16,32]{2,5,4,1,3,0:T(8,128)(2,1)} copy(bf16[1,4,49,3,16,32]{5,4,3,2,1,0:T(8,128)(2,1)S(1)} %reshape.602) | data formatting | bytes 1204224 | tf_op jit(solution)/shard_map/jit(_take)/gather | solution.py:46
  71.2 2.7 %broadcast_select_fusion = bf16[1,4,49,3,16,32]{2,5,4,1,3,0:T(8,128)(2,1)} fusion(bf16[1,4,49,3,16,32]{2,5,4,1,3,0:T(8,128)(2,1)} %copy.61, pred[4,49]{1,0:T(4,128)(4,1)S(1)} %broadcast_in_dim.101), kind=kLoop, calls=%fused_computation.29 | loop fusion | flops 301056 | bytes 1204420 | tf_op jit(solution)/shard_map/jit(_take)/select_n | solution.py:46
  76.1 2.1 %fusion.73 = (f32[4,16,49]{2,1,0:T(8,128)S(1)}, f32[4,16,49,49]{2,3,1,0:T(8,128)S(1)}) fusion(f32[16,49,49]{1,2,0:T(8,128)} %copy.63, bf16[1,4,49,3,16,32]{2,5,4,1,3,0:T(8,128)(2,1)} %broadcast_select_fusion, pred[4,49,49]{1,2,0:T(8,128)(4,1)S(1)} %copy.62), kind=kOutput, calls=%fused_computation.148 | convolution fusion | flops 10446016 | bytes 2144132 | tf_op jit(solution)/shard_map/bwihe,bwjhe->bwhij/dot_general | solution.py:58
  80.2 1.6 copy.86
  81.8 1.9 reshape.603
  88.0 3.6 %multiply_convert_fusion = (bf16[196,2048]{1,0:T(8,128)(2,1)S(1)}, f32[196,2048]{1,0:T(8,128)}) fusion(f32[2048]{0:T(1024)S(1)} %reshape.537, bf16[512,2048]{1,0:T(8,128)(2,1)} %bitcast.181, f32[196,512]{1,0:T(8,128)S(1)} %get-tuple-element.109, f32[512]{0:T(512)S(1)} %reshape.536, f32[512]{0:T(512)S(1)} %reshape.535, f32[196]{0:T(256)S(1)} %add_rsqrt_fusion, ...), kind=kOutput, calls=%fused_computation.27 | convolution fusion | flops 413952000 | bytes 4920864 | tf_op jit(solution)/shard_map/dot_general | solution.py:454
  91.7 3.5 %fusion.19 = bf16[1,196,512]{2,1,0:T(8,128)(2,1)} fusion(f32[196,512]{1,0:T(8,128)S(1)} %get-tuple-element.109, bf16[196,2048]{1,0:T(8,128)(2,1)S(1)} %get-tuple-element.110, bf16[512,2048]{1,0:T(8,128)(2,1)} %bitcast.183, f32[512]{0:T(512)S(1)} %reshape.538), kind=kOutput, calls=%fused_computation.50 | convolution fusion | flops 411342848 | bytes 3504128 | tf_op jit(solution)/shard_map/dot_general | solution.py:461
  95.1 2.7 %fusion.75 = (bf16[2048]{0:T(1024)(128)(2,1)S(1)}, bf16[196,2048]{1,0:T(8,128)(2,1)S(1)}) fusion(f32[196,2048]{1,0:T(8,128)} %get-tuple-element.111, bf16[512,2048]{1,0:T(8,128)(2,1)S(1)} %bitcast.184, bf16[1,196,512]{2,1,0:T(8,128)(2,1)S(1)} %copy-done.10), kind=kOutput, calls=%fused_computation.150 | convolution fusion | flops 415455232 | bytes 4710400 | tf_op jit(solution)/shard_map/dot_general | solution.py:517
  107.3 2.0 %pad_maximum_fusion = f32[1,4,49,3,16,32]{2,5,4,1,3,0:T(8,128)} fusion(f32[1,4,49,1,16,32]{2,5,4,1,3,0:T(8,128)S(1)} %convolution_bitcast_fusion.1, f32[1,4,49,1,16,32]{2,5,4,1,3,0:T(8,128)S(1)} %fusion.9, f32[1,4,49,1,16,32]{2,5,4,1,3,0:T(8,128)S(1)} %fusion.10), kind=kLoop, calls=%fused_computation.5 | loop fusion | flops 602112 | bytes 2408448 | tf_op jit(solution)/shard_map/stack | solution.py:558
  109.3 5.8 %copy.87 = f32[1,4,49,3,16,32]{5,4,3,2,1,0:T(8,128)} copy(f32[1,4,49,3,16,32]{2,5,4,1,3,0:T(8,128)} %pad_maximum_fusion) | data formatting | bytes 2408448 | tf_op jit(solution)/shard_map/reshape;reshape | solution.py:51
  115.1 4.0 %reshape.604 = f32[196,1536]{1,0:T(8,128)S(1)} reshape(f32[1,4,49,3,16,32]{5,4,3,2,1,0:T(8,128)} %copy.87) | data formatting | bytes 2408448 | tf_op jit(solution)/shard_map/reshape;reshape | solution.py:51
  120.5 2.3 %fusion.37 = (bf16[512]{0:T(512)(128)(2,1)S(1)}, f32[196]{0:T(256)S(1)}, f32[196]{0:T(256)S(1)}, bf16[512]{0:T(512)(128)(2,1)S(1)}, f32[196,512]{1,0:T(8,128)S(1)}) fusion(bf16[1,196,512]{2,1,0:T(8,128)(2,1)S(1)} %copy-done.5, f32[196]{0:T(256)S(1)} %copy-done.27, f32[196]{0:T(256)S(1)} %copy-done.21, f32[512]{0:T(512)S(1)} %reshape.530, ...), kind=kOutput, calls=%fused_computation.76 | convolution fusion | flops 309584512 | bytes 3386628 | tf_op jit(solution)/shard_map/dot_general | solution.py:566
  124.2 2.1 %convolution_convert_fusion.1 = bf16[2048,512]{0,1:T(8,128)(2,1)} fusion(bf16[196,2048]{1,0:T(8,128)(2,1)S(1)} %copy-done.3, bf16[1,196,512]{2,1,0:T(8,128)(2,1)S(1)} %copy-done.11), kind=kOutput, calls=%fused_computation.7 | convolution fusion | flops 412090368 | bytes 3100672 | tf_op jit(solution)/shard_map/dot_general | solution.py:515
  126.3 2.2 %convolution_convert_fusion = bf16[512,2048]{1,0:T(8,128)(2,1)} fusion(bf16[196,2048]{1,0:T(8,128)(2,1)S(1)} %copy-done.16, f32[196,512]{1,0:T(8,128)S(1)} %get-tuple-element.109, f32[512]{0:T(512)S(1)} %reshape.536, f32[512]{0:T(512)S(1)} %reshape.535, f32[196]{0:T(256)S(1)} %add_rsqrt_fusion, f32[196]{0:T(256)S(1)} %broadcast_multiply_fusion.4), kind=kOutput, calls=%fused_computation.6 | convolution fusion | flops 412592128 | bytes 3307040 | tf_op jit(solution)/shard_map/dot_general | solution.py:519
  128.5 1.9 convolution_convert_fusion.2
  133.5 1.9 fusion.11
  136.1 48.1 %scatter_parts.1 = (f32[16,2048]{1,0:T(8,128)}, f32[16,2048]{1,0:T(8,128)}, f32[16,1536]{1,0:T(8,128)}, f32[16,640]{1,0:T(8,128)}, f32[24,128]{1,0:T(8,128)}) custom-call(bf16[16,2,1,16,2048]{4,3,2,1,0:T(8,128)(2,1)} %bitcast.176, bf16[16,2,1,16,2048]{4,3,2,1,0:T(8,128)(2,1)} %bitcast.177, bf16[16,2,1,16,1536]{4,3,2,1,0:T(8,128)(2,1)} %bitcast.178, ...), custom_call_target="tpu_custom_call" | custom-call | tf_op jit(solution)/shard_map/scatter_parts/pallas_call | solution.py:261
  189.5 1.5 copy.103
  191.1 1.6 copy.104
  192.6 1.6 copy.105
  (171 shorter events, 35.0 us)
Async XLA Ops:
  0.6 73.5 %copy-start = (bf16[169,16]{0,1:T(8,128)(2,1)S(1)}, bf16[169,16]{0,1:T(8,128)(2,1)}, u32[]{:S(2)}) copy-start(bf16[169,16]{0,1:T(8,128)(2,1)} %param.32) | copy-start | bytes 16228
  0.7 61.0 %copy-start.4 = (bf16[1,196,512]{2,1,0:T(8,128)(2,1)S(1)}, bf16[1,196,512]{2,1,0:T(8,128)(2,1)}, u32[]{:S(2)}) copy-start(bf16[1,196,512]{2,1,0:T(8,128)(2,1)} %param.18) | copy-start | bytes 602116
  58.9 3.2 %copy-start.37 = (bf16[2,2,2,2,2,16,1536]{6,5,4,3,2,1,0:T(8,128)(2,1)S(1)}, bf16[2,2,2,2,2,16,1536]{6,5,4,3,2,1,0:T(8,128)(2,1)}, u32[]{:S(2)}) copy-start(bf16[2,2,2,2,2,16,1536]{6,5,4,3,2,1,0:T(8,128)(2,1)} %get-tuple-element.25) | copy-start | bytes 4718596
  59.9 2.1 %copy-start.17 = (bf16[4,8,16,128]{3,1,2,0:T(8,128)(2,1)}, bf16[4,8,16,128]{3,1,2,0:T(8,128)(2,1)S(1)}, u32[]{:S(2)}) copy-start(bf16[4,8,16,128]{3,1,2,0:T(8,128)(2,1)S(1)} %copy.99) | copy-start | bytes 393220
  61.2 25.0 %copy-start.6 = (bf16[32,16,512]{2,1,0:T(8,128)(2,1)}, bf16[32,16,512]{2,1,0:T(8,128)(2,1)S(1)}, u32[]{:S(2)}) copy-start(bf16[32,16,512]{2,1,0:T(8,128)(2,1)S(1)} %slice.152) | copy-start | bytes 1572868
  61.6 3.0 %copy-start.28 = (f32[512]{0:T(512)}, f32[512]{0:T(512)S(1)}, u32[]{:S(2)}) copy-start(f32[512]{0:T(512)S(1)} %reshape.531) | copy-start | bytes 6148
  61.8 2.8 %copy-start.20 = (f32[196]{0:T(256)}, f32[196]{0:T(256)S(1)}, u32[]{:S(2)}) copy-start(f32[196]{0:T(256)S(1)} %broadcast_multiply_fusion.5) | copy-start | bytes 2356
  62.6 2.0 %copy-start.32 = (s32[196]{0:T(256)}, s32[196]{0:T(256)S(1)}, u32[]{:S(2)}) copy-start(s32[196]{0:T(256)S(1)} %compare_select_fusion.1) | copy-start | bytes 2356
  62.7 2.0 %copy-start.24 = (s32[1024]{0:T(1024)}, s32[1024]{0:T(1024)S(1)}, u32[]{:S(2)}) copy-start(s32[1024]{0:T(1024)S(1)} %pad_clamp_fusion.1) | copy-start | bytes 12292
  70.6 3.4 %copy-start.19 = (s32[49,49]{1,0:T(8,128)S(1)}, s32[49,49]{1,0:T(8,128)}, u32[]{:S(2)}) copy-start(s32[49,49]{1,0:T(8,128)} %param.34) | copy-start | bytes 28816
  74.0 2.0 %copy-start.18 = (s32[4,49,49]{2,0,1:T(4,128)S(1)}, s32[4,49,49]{2,0,1:T(4,128)}, u32[]{:S(2)}) copy-start(s32[4,49,49]{2,0,1:T(4,128)} %param.33) | copy-start | bytes 115252
  74.1 4.1 %copy-start.22 = (s32[2401]{0:T(1024)}, s32[2401]{0:T(1024)S(1)}, u32[]{:S(2)}) copy-start(s32[2401]{0:T(1024)S(1)} %eq.23) | copy-start | bytes 28816
  85.2 2.5 %copy-start.25 = (s32[1024]{0:T(1024)}, s32[1024]{0:T(1024)S(1)}, u32[]{:S(2)}) copy-start(s32[1024]{0:T(1024)S(1)} %pad_clamp_fusion) | copy-start | bytes 12292
  86.2 5.3 %copy-start.12 = (bf16[196,512]{1,0:T(8,128)(2,1)}, bf16[196,512]{1,0:T(8,128)(2,1)S(1)}, u32[]{:S(2)}) copy-start(bf16[196,512]{1,0:T(8,128)(2,1)S(1)} %gather_fusion.1) | copy-start | bytes 602116
  86.3 1.7 copy-start.30
  91.6 3.5 %copy-start.2 = (bf16[196,2048]{1,0:T(8,128)(2,1)}, bf16[196,2048]{1,0:T(8,128)(2,1)S(1)}, u32[]{:S(2)}) copy-start(bf16[196,2048]{1,0:T(8,128)(2,1)S(1)} %get-tuple-element.110) | copy-start | bytes 2408452
  91.7 3.5 %copy-start.9 = (bf16[2,2,2,2,2,16,2048]{6,5,4,3,2,1,0:T(8,128)(2,1)S(1)}, bf16[2,2,2,2,2,16,2048]{6,5,4,3,2,1,0:T(8,128)(2,1)}, u32[]{:S(2)}) copy-start(bf16[2,2,2,2,2,16,2048]{6,5,4,3,2,1,0:T(8,128)(2,1)} %get-tuple-element.27) | copy-start | bytes 6291460
  91.7 3.5 %copy-start.10 = (bf16[1,196,512]{2,1,0:T(8,128)(2,1)S(1)}, bf16[1,196,512]{2,1,0:T(8,128)(2,1)}, u32[]{:S(2)}) copy-start(bf16[1,196,512]{2,1,0:T(8,128)(2,1)} %param.19) | copy-start | bytes 602116
  95.1 2.8 %copy-start.8 = (bf16[2,2,2,2,2,16,2048]{6,5,4,3,2,1,0:T(8,128)(2,1)S(1)}, bf16[2,2,2,2,2,16,2048]{6,5,4,3,2,1,0:T(8,128)(2,1)}, u32[]{:S(2)}) copy-start(bf16[2,2,2,2,2,16,2048]{6,5,4,3,2,1,0:T(8,128)(2,1)} %get-tuple-element.26) | copy-start | bytes 6291460
  100.7 1.7 copy-start.34
  124.2 2.1 %copy-start.16 = (bf16[196,2048]{1,0:T(8,128)(2,1)S(1)}, bf16[196,2048]{1,0:T(8,128)(2,1)}, u32[]{:S(2)}) copy-start(bf16[196,2048]{1,0:T(8,128)(2,1)} %copy-done.15) | copy-start | bytes 2408452
  126.3 2.2 %copy-start.29 = (f32[512]{0:T(512)S(1)}, f32[512]{0:T(512)}, u32[]{:S(2)}) copy-start(f32[512]{0:T(512)} %copy-done.28) | copy-start | bytes 6148
  128.5 2.6 %copy-start.35 = (bf16[512]{0:T(512)(128)(2,1)S(1)}, bf16[512]{0:T(512)(128)(2,1)}, u32[]{:S(2)}) copy-start(bf16[512]{0:T(512)(128)(2,1)} %get-tuple-element.78) | copy-start | bytes 3076
  130.8 2.2 %copy-start.14 = (f32[16,49,49]{1,2,0:T(8,128)S(1)}, f32[16,49,49]{1,2,0:T(8,128)}, u32[]{:S(2)}) copy-start(f32[16,49,49]{1,2,0:T(8,128)} %get-tuple-element.86) | copy-start | bytes 460996
  (14 other events, 17.4 us)

commit v2 on v1

--- a/solution.py
+++ b/solution.py
@@ -42,26 +42,162 @@
     return (pre_act * normal_cdf, normal_cdf + pre_act * normal_pdf)
 
 
-def to_windows(token_rows, partition):
-    picked = jnp.take(token_rows, partition, axis=1)
-    return picked.reshape(token_rows.shape[0], WIN_IMG, WINDOW, token_rows.shape[-1])
-
-
-def from_windows(window_rows, inverse):
-    flat_rows = window_rows.reshape(window_rows.shape[0], inverse.shape[0], window_rows.shape[-1])
-    return jnp.take(flat_rows, inverse, axis=1)
-
-
-def window_scores(queries, key_rows, lookups, score_scale):
-    table_bias, allowed, partition, inverse = lookups
-    raw = (
-        jnp.einsum("bwihe,bwjhe->bwhij", queries, key_rows, preferred_element_type=jnp.float32)
-        * score_scale
-        + table_bias
-    )
-    return jnp.where(allowed, raw, NEG_FILL)
-
-
+NT = (((1,), (1,)), ((), ()))
+TN = (((0,), (0,)), ((), ()))
+
+
+def mul(left, right, dims=(((1,), (0,)), ((), ()))):
+    return lax.dot_general(left, right, dims, preferred_element_type=jnp.float32)
+
+
+def pair_mask(mask_ref, spread, same_ref):
+    return (mul(mask_ref[...], spread) > 0.5) & (same_ref[...] > 0)
+
+
+def head_scores(query, key_block, bias, spread_t, spread, allowed, scale):
+    wide = mul(mul(spread_t, bias).astype(jnp.bfloat16), spread)
+    return jnp.where(allowed, mul(query, key_block, NT) * scale + wide, NEG_FILL)
+
+
+def soft_rows(scores):
+    row_top = jnp.max(scores, axis=-1, keepdims=True)
+    log_total = row_top + jnp.log(jnp.sum(jnp.exp(scores - row_top), axis=-1, keepdims=True))
+    return jnp.exp(scores - log_total)
+
+
+def head_lanes(rows, lanes, width, h):
+    lane = lax.broadcasted_iota(jnp.int32, (rows, lanes), 1)
+    return (lane >= h * width) & (lane < (h + 1) * width)
+
+
+def attend_kernel(
+    width, qkv_ref, pick_ref, back_ref, bias_ref, mask_ref, same_ref, spread_ref, spread_t_ref,
+    qkv_win_ref, out_ref
+):
+    rows, model = out_ref.shape
+    spread, spread_t = spread_ref[...], spread_t_ref[...]
+    allowed = pair_mask(mask_ref, spread, same_ref)
+    qkv_win_ref[...] = mul(pick_ref[...], qkv_ref[...]).astype(jnp.bfloat16)
+    heads = LANES // width
+    for group in range(model // LANES):
+        low = group * LANES
+        query = qkv_win_ref[:, low : low + LANES]
+        keys = qkv_win_ref[:, model + low : model + low + LANES]
+        values = qkv_win_ref[:, 2 * model + low : 2 * model + low + LANES]
+        total = jnp.zeros((rows, LANES), jnp.float32)
+        for h in range(heads):
+            lanes = head_lanes(rows, LANES, width, h)
+            scores = head_scores(
+                jnp.where(lanes, query, jnp.zeros_like(query)),
+                keys,
+                bias_ref[group * heads + h],
+                spread_t,
+                spread,
+                allowed,
+                width ** (-0.5),
+            )
+            probs = soft_rows(scores).astype(jnp.bfloat16)
+            total = jnp.where(lanes, mul(probs, values), total)
+        out_ref[:, low : low + LANES] = mul(back_ref[...], total.astype(jnp.bfloat16)).astype(
+            jnp.bfloat16
+        )
+
+
+def attend_back_kernel(
+    width, qkv_win_ref, grad_ref, pick_ref, back_ref, bias_ref, mask_ref, same_ref, spread_ref,
+    spread_t_ref, out_ref, sums_ref, pair_ref
+):
+    rows, model = grad_ref.shape
+    spread, spread_t = spread_ref[...], spread_t_ref[...]
+    allowed = pair_mask(mask_ref, spread, same_ref)
+    heads = LANES // width
+    scale = width ** (-0.5)
+    for group in range(model // LANES):
+        low = group * LANES
+        query = qkv_win_ref[:, low : low + LANES]
+        keys = qkv_win_ref[:, model + low : model + low + LANES]
+        values = qkv_win_ref[:, 2 * model + low : 2 * model + low + LANES]
+        grad = mul(pick_ref[...], grad_ref[:, low : low + LANES]).astype(jnp.bfloat16)
+        totals = [jnp.zeros((rows, LANES), jnp.float32) for _ in range(3)]
+        for h in range(heads):
+            lanes = head_lanes(rows, LANES, width, h)
+            scores = head_scores(
+                jnp.where(lanes, query, jnp.zeros_like(query)),
+                keys,
+                bias_ref[group * heads + h],
+                spread_t,
+                spread,
+                allowed,
+                scale,
+            )
+            soft = soft_rows(scores)
+            prob_grad = mul(jnp.where(lanes, grad, jnp.zeros_like(grad)), values, NT)
+            inner = jnp.sum(soft * prob_grad, axis=-1, keepdims=True)
+            score_grad = soft * (prob_grad - inner)
+            coarse = score_grad.astype(jnp.bfloat16)
+            fine = (score_grad - coarse.astype(jnp.float32)).astype(jnp.bfloat16)
+            pair = jnp.zeros(pair_ref.shape[1:], jnp.float32)
+            for piece in (coarse, fine):
+                pair += mul(mul(spread, piece).astype(jnp.bfloat16), spread_t)
+            pair_ref[group * heads + h] = pair
+            totals[0] = jnp.where(lanes, mul(coarse, keys) * scale, totals[0])
+            totals[1] = jnp.where(lanes, mul(coarse, query, TN) * scale, totals[1])
+            totals[2] = jnp.where(lanes, mul(soft.astype(jnp.bfloat16), grad, TN), totals[2])
+        for k in range(3):
+            at = k * model + low
+            sums_ref[:, at : at + LANES] = jnp.sum(totals[k], axis=0, keepdims=True)
+            out_ref[:, at : at + LANES] = mul(
+                back_ref[...], totals[k].astype(jnp.bfloat16)
+            ).astype(jnp.bfloat16)
+
+
+def attention_tables(bias_heads, window_mask, partition):
+    tokens = partition.shape[0]
+    span = window_mask.shape[-1]
+    token = jnp.arange(tokens, dtype=jnp.int32)
+    pick = (partition[:, None] == token[None, :]).astype(jnp.bfloat16)
+    back = (partition[None, :] == token[:, None]).astype(jnp.bfloat16)
+    same = (token[:, None] // span == token[None, :] // span).astype(jnp.float32)
+    spread = (token[None, :] % span == jnp.arange(span)[:, None]).astype(jnp.bfloat16)
+    mask_rows = (window_mask == 1).astype(jnp.bfloat16).reshape(tokens, span)
+    return (pick, back, bias_heads.astype(jnp.bfloat16), mask_rows, same, spread, spread.T)
+
+
+def attend(qkv_rows, tables):
+    rows, wide = qkv_rows.shape
+    model = wide // 3
+    spec = pl.BlockSpec(memory_space=pltpu.VMEM)
+    return pl.pallas_call(
+        functools.partial(attend_kernel, model // HEADS),
+        out_shape=[
+            jax.ShapeDtypeStruct((rows, wide), jnp.bfloat16),
+            jax.ShapeDtypeStruct((rows, model), jnp.bfloat16),
+        ],
+        in_specs=[spec] * 8,
+        out_specs=[spec] * 2,
+        name="attend",
+    )(qkv_rows, *tables)
+
+
+def attend_back(qkv_win, grad_att, tables):
+    rows, wide = qkv_win.shape
+    model = wide // 3
+    span = tables[3].shape[1]
+    spec = pl.BlockSpec(memory_space=pltpu.VMEM)
+    return pl.pallas_call(
+        functools.partial(attend_back_kernel, model // HEADS),
+        out_shape=[
+            jax.ShapeDtypeStruct((rows, wide), jnp.bfloat16),
+            jax.ShapeDtypeStruct((1, wide), jnp.float32),
+            jax.ShapeDtypeStruct((HEADS, span, span), jnp.float32),
+        ],
+        in_specs=[spec] * 9,
+        out_specs=[spec] * 3,
+        name="attend_back",
+    )(qkv_win, grad_att, *tables)
+
+
+LANES = 128
 MESH = pl.DeviceIdType.MESH
 
 
@@ -153,11 +289,12 @@
     return [out.reshape((count,) + part.shape) for out, part in zip(outs, parts)]
 
 
-def scatter_kernel(bit_count, part_count, *refs):
+def scatter_kernel(bit_count, part_count, split, vector_count, *refs):
     count = 1 << bit_count
     ins, table_in = refs[:part_count], refs[part_count]
     outs, table_out = refs[part_count + 1 : 2 * part_count + 1], refs[2 * part_count + 1]
-    rest = list(refs[2 * part_count + 2 :])
+    vector_outs = refs[2 * part_count + 2 : 2 * part_count + 2 + vector_count]
+    rest = list(refs[2 * part_count + 2 + vector_count :])
     send_sem, recv_sem, table_send, table_recv = rest[:4]
     table_got, table_sum = rest[4:6]
     got = rest[6 : 6 + part_count * bit_count]
@@ -205,7 +342,13 @@
             return source[i, mine[bit], j].astype(jnp.float32) + arrived[i, j].astype(jnp.float32)
 
         if step == bit_count - 1:
-            outs[p][...] = total(0)
+            final = total(0)
+            outs[p][...] = final[:, : outs[p].shape[1]]
+            if p == part_count - 1:
+                for k in range(vector_count):
+                    vector_outs[k][...] = final[
+                        k : k + 1, split : split + vector_outs[k].shape[1]
+                    ]
             return
         target = held[p * (bit_count - 1) + step]
         low_next = target.shape[2]
@@ -243,7 +386,7 @@
     return (1 << (len(left) - 1 - place_of), 2, 1 << place_of)
 
 
-def scatter_parts(parts, table, count):
+def scatter_parts(parts, table, count, split, lengths):
     bit_count = count.bit_length() - 1
     part_count = len(parts)
     spec = pl.BlockSpec(memory_space=pltpu.VMEM)
@@ -259,11 +402,15 @@
             else:
                 held.append(pltpu.VMEM((high, two, low) + block, part.dtype))
     outs = pl.pallas_call(
-        functools.partial(scatter_kernel, bit_count, part_count),
-        out_shape=[jax.ShapeDtypeStruct(part.shape[1:], jnp.float32) for part in parts]
-        + [jax.ShapeDtypeStruct(table.shape, jnp.float32)],
+        functools.partial(scatter_kernel, bit_count, part_count, split, len(lengths)),
+        out_shape=[jax.ShapeDtypeStruct(part.shape[1:], jnp.float32) for part in parts[:-1]]
+        + [
+            jax.ShapeDtypeStruct((parts[-1].shape[1], split), jnp.float32),
+            jax.ShapeDtypeStruct(table.shape, jnp.float32),
+        ]
+        + [jax.ShapeDtypeStruct((1, length), jnp.float32) for length in lengths],
         in_specs=[spec] * (part_count + 1),
-        out_specs=[spec] * (part_count + 1),
+        out_specs=[spec] * (part_count + 1 + len(lengths)),
         scratch_shapes=[
             pltpu.SemaphoreType.DMA((part_count, bit_count)),
             pltpu.SemaphoreType.DMA((part_count, bit_count)),
@@ -277,10 +424,9 @@
         compiler_params=pltpu.CompilerParams(collective_id=1, has_side_effects=True),
         name="scatter_parts",
     )(*shaped, table)
-    return (outs[:part_count], outs[part_count])
-
-
-LANES = 128
+    return (outs[:part_count], outs[part_count + 1 :], outs[part_count])
+
+
 ROWS = 16
 
 
@@ -294,12 +440,19 @@
     return blocks[..., : r * c // blocks.shape[-2]].reshape(blocks.shape[:-2] + (r, c))
 
 
-def with_vectors(block, flat):
-    rows, width = block.shape[-2:]
-    extra = -(-flat.shape[-1] // rows)
-    total = -(-(width + extra) // LANES) * LANES - width
-    padded = jnp.pad(flat, [(0, 0)] * (flat.ndim - 1) + [(0, rows * total - flat.shape[-1])])
-    return jnp.concatenate([block, padded.reshape(flat.shape[:-1] + (rows, total))], axis=-1)
+def vector_rows(vectors, like):
+    rows, width = like.shape[-2:]
+    longest = max(v.shape[-1] for v in vectors)
+    total = -(-(width + longest) // LANES) * LANES - width
+    tile = jnp.zeros(like.shape[:-1] + (total,), like.dtype)
+    lead = [(0, 0)] * (like.ndim - 2)
+    for k, v in enumerate(vectors):
+        tile += jnp.pad(v[..., None, :], lead + [(k, rows - 1 - k), (0, total - v.shape[-1])])
+    return tile
+
+
+def with_vectors(block, vectors):
+    return jnp.concatenate([block, vector_rows(vectors, block)], axis=-1)
 
 
 def fetch_all(shards):
@@ -312,7 +465,7 @@
         fold(fc1),
         fold(fc2_t),
         fold(qkv),
-        with_vectors(folded_proj, jnp.concatenate(vectors)),
+        with_vectors(folded_proj, vectors),
     ]
     fc1_all, fc2_all, qkv_all, proj_all = gather_parts(parts, count)
 
@@ -320,11 +473,10 @@
         r, c = shard.shape
         return unfold(blocks, r, c).reshape(count * r, c)
 
-    flat = proj_all[:, :, folded_proj.shape[1] :].reshape(count, -1)
-    start, gathered = 0, []
-    for length in lengths:
-        gathered.append(flat[:, start : start + length].reshape(-1))
-        start += length
+    at = folded_proj.shape[1]
+    gathered = [
+        proj_all[:, k, at : at + length].reshape(-1) for k, length in enumerate(lengths)
+    ]
     return (
         gathered[0],
         gathered[1],
@@ -355,23 +507,21 @@
         blocks(grads[10]),
         blocks(grads[8]),
         blocks(grads[2]),
-        with_vectors(folded_proj, jnp.concatenate(vectors, axis=1)),
+        with_vectors(folded_proj, vectors),
     ]
     entries = table_local.size
     table_rows = -(-entries // (8 * LANES)) * 8
     table_pad = jnp.pad(table_local.reshape(-1), (0, table_rows * LANES - entries)).reshape(
         table_rows, LANES
     )
-    (fc2_b, fc1_b, qkv_b, proj_b), table_sum = scatter_parts(parts, table_pad, count)
+    (fc2_b, fc1_b, qkv_b, proj_b), vector_outs, table_sum = scatter_parts(
+        parts, table_pad, count, folded_proj.shape[2], [v.shape[1] for v in vectors]
+    )
 
     def own(block, grad):
         return unfold(block, grad.shape[0] // count, grad.shape[1])
 
-    flat = proj_b[:, folded_proj.shape[2] :].reshape(-1)
-    start, pieces = 0, []
-    for vector in vectors:
-        pieces.append(flat[start : start + vector.shape[1]])
-        start += vector.shape[1]
+    pieces = [piece[0] for piece in vector_outs]
     table_grad = table_sum.reshape(-1)[:entries].reshape(table_local.shape)
     return (
         (
@@ -407,11 +557,8 @@
         fc2_weight,
         fc2_bias,
     ) = params
-    table_bias, allowed, partition, inverse = lookups
     image_count, tok_count, model_width = images.shape
     row_count = image_count * tok_count
-    head_width = model_width // HEADS
-    score_scale = head_width ** (-0.5)
     inputs_f = images.astype(jnp.float32).reshape(row_count, model_width)
     normed_one, unit_one, inv_one = normalize(
         inputs_f, gain_one.astype(jnp.float32), shift_one.astype(jnp.float32)
@@ -427,21 +574,7 @@
     qkv_rows = (
         jnp.dot(normed_one, qkv_weight, preferred_element_type=jnp.float32) + qkv_shift
     ).astype(jnp.bfloat16)
-    qkv_win = to_windows(
-        qkv_rows.reshape(image_count, tok_count, 3 * model_width), partition
-    ).reshape(image_count, WIN_IMG, WINDOW, 3, HEADS, head_width)
-    scores = window_scores(qkv_win[:, :, :, 0], qkv_win[:, :, :, 1], lookups, score_scale)
-    row_top = jnp.max(scores, axis=-1, keepdims=True)
-    log_total = row_top + jnp.log(jnp.sum(jnp.exp(scores - row_top), axis=-1, keepdims=True))
-    soft_probs = jnp.exp(scores - log_total).astype(jnp.bfloat16)
-    mixed = jnp.einsum(
-        "bwhij,bwjhe->bwihe", soft_probs, qkv_win[:, :, :, 2], preferred_element_type=jnp.float32
-    )
-    attended = (
-        from_windows(mixed.reshape(image_count, WIN_IMG, WINDOW, model_width), inverse)
-        .astype(jnp.bfloat16)
-        .reshape(row_count, model_width)
-    )
+    qkv_win, attended = attend(qkv_rows, lookups)
     resid = (
         inputs_f
         + jnp.dot(attended, proj_weight, preferred_element_type=jnp.float32)
@@ -466,7 +599,6 @@
         inv_one,
         normed_one,
         qkv_win,
-        log_total,
         attended,
         unit_two,
         inv_two,
@@ -497,7 +629,6 @@
         inv_one,
         normed_one,
         qkv_win,
-        log_total,
         attended,
         unit_two,
         inv_two,
@@ -505,11 +636,8 @@
         gelu_slope,
         activ,
     ) = saved
-    table_bias, allowed, partition, inverse = lookups
     image_count, tok_count, model_width = cotangent.shape
     row_count = image_count * tok_count
-    head_width = model_width // HEADS
-    score_scale = head_width ** (-0.5)
     cot_rows = cotangent.reshape(row_count, model_width)
     cot_f = cot_rows.astype(jnp.float32)
     fc2_grad = jnp.dot(cot_rows.T, activ, preferred_element_type=jnp.float32)
@@ -529,39 +657,9 @@
     grad_att = jnp.dot(grad_resid_b, proj_weight.T, preferred_element_type=jnp.float32).astype(
         jnp.bfloat16
     )
-    grad_mixed = to_windows(
-        grad_att.reshape(image_count, tok_count, model_width), partition
-    ).reshape(image_count, WIN_IMG, WINDOW, HEADS, head_width)
-    queries = qkv_win[:, :, :, 0]
-    key_rows = qkv_win[:, :, :, 1]
-    value_rows = qkv_win[:, :, :, 2]
-    scores = window_scores(queries, key_rows, lookups, score_scale)
-    soft_full = jnp.exp(scores - log_total)
-    soft_probs = soft_full.astype(jnp.bfloat16)
-    value_grad = jnp.einsum(
-        "bwhij,bwihe->bwjhe", soft_probs, grad_mixed, preferred_element_type=jnp.float32
-    )
-    prob_grad = jnp.einsum(
-        "bwihe,bwjhe->bwhij", grad_mixed, value_rows, preferred_element_type=jnp.float32
-    )
-    score_grad = soft_full * (prob_grad - jnp.sum(soft_full * prob_grad, axis=-1, keepdims=True))
-    pair_grad = jnp.sum(score_grad, axis=(0, 1))
-    score_grad_b = score_grad.astype(jnp.bfloat16)
-    query_grad = (
-        jnp.einsum("bwhij,bwjhe->bwihe", score_grad_b, key_rows, preferred_element_type=jnp.float32)
-        * score_scale
-    )
-    key_grad = (
-        jnp.einsum("bwhij,bwihe->bwjhe", score_grad_b, queries, preferred_element_type=jnp.float32)
-        * score_scale
-    )
-    stacked = jnp.stack([query_grad, key_grad, value_grad], axis=3).reshape(
-        image_count, WIN_IMG, WINDOW, 3 * model_width
-    )
-    qkv_grad = from_windows(stacked, inverse).reshape(row_count, 3 * model_width)
-    qkv_grad_b = qkv_grad.astype(jnp.bfloat16)
+    qkv_grad_b, column_sums, pair_grad = attend_back(qkv_win, grad_att, lookups)
+    column_sums = column_sums[0]
     qkv_grad_w = jnp.dot(normed_one.T, qkv_grad_b, preferred_element_type=jnp.float32)
-    column_sums = jnp.sum(qkv_grad, axis=0)
     qv_grad = jnp.concatenate([column_sums[:model_width], column_sums[2 * model_width :]])
     grad_first = jnp.dot(qkv_grad_b, qkv_weight.T, preferred_element_type=jnp.float32)
     grad_low, gain_one_grad, shift_one_grad = norm_backward(
@@ -630,12 +728,7 @@
         ),
         (2, 0, 1),
     )
-    allowed = (window_mask == 1)[None, :, None, :, :]
-    tok_count = partition.shape[0]
-    inverse = (
-        jnp.zeros((tok_count,), jnp.int32).at[partition].set(jnp.arange(tok_count, dtype=jnp.int32))
-    )
-    lookups = (table_bias, allowed, partition, inverse)
+    lookups = attention_tables(table_bias, window_mask, partition)
     held_params = fetch_all(shards)
     micro_index = 0
     output, saved = forward_pass(block_input, held_params, lookups)

time: 195 us -> 193 us (0.990)
  Pallas kernels: 99.5 us -> 125 us
  local copies, waits for them, and re-layouts: 52.1 us -> 26.7 us
  matrix products: 29.8 us -> 26 us
    pallas_call x1 -> x3, Pallas kernels: 48.1 us -> 73.4 us  [the longest x1 48.2 us: scatter_parts(): pl.pallas_call(functools.partial(scatter_kernel, bit_count, part_count, s...]
    another operation x4 -> x1, local copies, waits for them, and re-layouts: 13.2 us -> 0.68 us  [vector_rows(): v[..., None, :]]
    gather x8 -> x0, local copies, waits for them, and re-layouts: 12 us -> none  [the longest x6 9.64 us: to_windows(): picked = jnp.take(token_rows, partition, axis=1)]
    unnamed x84 -> x92, local copies, waits for them, and re-layouts: 8.88 us -> 17.4 us
    dot_general x6 -> x0, matrix products: 5.88 us -> none  [the longest x1 2.06 us: window_scores(): jnp.einsum('bwihe,bwjhe->bwhij', queries, key_rows, preferred_element_typ...]
    concatenate x2 -> x0, local copies, waits for them, and re-layouts: 5.58 us -> none  [the longest x1 5.47 us: fetch_all(): jnp.concatenate(vectors)]
    select_n x4 -> x2, other arithmetic: 2.98 us -> 0.02 us  [the longest x1 0.01 us: attention_tables(): token[:, None] // span == token[None, :] // span]
    dot_general x1, matrix products: 0.55 us -> 2.81 us  [forward_pass(): jnp.dot(normed_one, qkv_weight, preferred_element_type=jnp.float32)]
where the time goes in v2:
time: 193 us; the launch traced here: 192 us
  Pallas kernels  125 us (65%)
  local copies, waits for them, and re-layouts  26.7 us (14%)
  matrix products  26 us (13%)
  other arithmetic  13.2 us (7%)
    pallas_call x1, Pallas kernels, gather_parts(): pl.pallas_call(functools.partial(gather_kernel, bit_count, part_count), o...  51.2 us
    pallas_call x1, Pallas kernels, scatter_parts(): pl.pallas_call(functools.partial(scatter_kernel, bit_count, part_count, s...  48.2 us
    unnamed x92, local copies, waits for them, and re-layouts  17.4 us
    pallas_call x1, Pallas kernels, attend_back(): pl.pallas_call(functools.partial(attend_back_kernel, model // HEADS), out...  15.7 us
    pallas_call x1, Pallas kernels, attend(): pl.pallas_call(functools.partial(attend_kernel, model // HEADS), out_shap...  9.45 us

profile of v2, /device:TPU:0, one launch (start us, length us, event | category | flops | bytes accessed | tf_op | source)
XLA Modules:
  0.0 191.8 jit_solution(9724890209811721176)
XLA Ops:
  6.3 1.3 pad_maximum_fusion.1.refs_3_
  12.8 51.2 %gather_parts.1 = (bf16[2,2,2,2,2,16,2048]{6,5,4,3,2,1,0:T(8,128)(2,1)}, bf16[2,2,2,2,2,16,2048]{6,5,4,3,2,1,0:T(8,128)(2,1)}, bf16[2,2,2,2,2,16,1536]{6,5,4,3,2...) custom-call(bf16[16,2048]{1,0:T(8,128)(2,1)} %refs_0_.1, bf16[16,2048]{1,0:T(8,128)(2,1)} %bitcast.144, ...), custom_call_target="tpu_custom_call" | custom-call | tf_op jit(solution)/shard_map/gather_parts/pallas_call | solution.py:274
  66.1 1.4 fusion.76
  69.1 2.8 %fusion.1.qkv_ref = bf16[196,1536]{1,0:T(8,128)(2,1)} fusion(bf16[512,1536]{1,0:T(8,128)(2,1)} %bitcast.153, f32[1536]{0:T(1024)S(1)} %pad_maximum_fusion.2, bf16[1,196,512]{2,1,0:T(8,128)(2,1)S(1)} %copy-done.1, f32[512]{0:T(512)S(1)} %reshape.371, f32[512]{0:T(512)S(1)} %reshape.370, f32[196]{0:T(256)S(1)} %add_rsqrt_fusion.1, ...), kind=kOutput, calls=%fused_computation.8 | convolution fusion | flops 309485568 | bytes 2387488 | tf_op jit(solution)/shard_map/dot_general | solution.py:575
  71.9 9.5 %attend.1 = (bf16[196,1536]{1,0:T(8,128)(2,1)}, bf16[196,512]{1,0:T(8,128)(2,1)}) custom-call(bf16[196,1536]{1,0:T(8,128)(2,1)} %fusion.1.qkv_ref, bf16[196,196]{1,0:T(8,128)(2,1)} %get-tuple-element.110.pick_ref, bf16[196,196]{1,0:T(8,128)(2,1)} %get-tuple-element.109.back_ref, bf16[16,49,49]{2,1,0:T(8,128)(2,1)} %bitcast.135, ...), custom_call_target="tpu_custom_call" | custom-call | tf_op jit(solution)/shard_map/attend/pallas_call | solution.py:170
  81.3 1.3 fusion.77
  82.9 2.6 %multiply_convert_fusion = (bf16[196,2048]{1,0:T(8,128)(2,1)S(1)}, f32[196,2048]{1,0:T(8,128)S(1)}) fusion(f32[2048]{0:T(1024)S(1)} %reshape.379, bf16[512,2048]{1,0:T(8,128)(2,1)} %bitcast.130, f32[196,512]{1,0:T(8,128)S(1)} %get-tuple-element.112, f32[512]{0:T(512)S(1)} %reshape.378, f32[512]{0:T(512)S(1)} %reshape.377, f32[196]{0:T(256)S(1)} %add_rsqrt_fusion, ...), kind=kOutput, calls=%fused_computation.16 | convolution fusion | flops 413952000 | bytes 4920864 | tf_op jit(solution)/shard_map/dot_general | solution.py:587
  85.5 1.8 fusion.78
  87.2 1.5 fusion.14
  88.8 1.5 multiply_reduce_fusion
  92.1 15.7 %attend_back.1 = (bf16[196,1536]{1,0:T(8,128)(2,1)}, f32[1,1536]{1,0:T(1,128)}, f32[16,49,49]{2,1,0:T(8,128)}) custom-call(bf16[196,1536]{1,0:T(8,128)(2,1)} %get-tuple-element.42.qkv_win_ref, bf16[196,512]{1,0:T(8,128)(2,1)} %convolution_convert_fusion.5.grad_ref, bf16[196,196]{1,0:T(8,128)(2,1)} %get-tuple-element.110.pick_ref, ...), custom_call_target="tpu_custom_call" | custom-call | tf_op jit(solution)/shard_map/attend_back/pallas_call | solution.py:187
  107.9 3.6 %fusion.29 = (bf16[512]{0:T(512)(128)(2,1)}, f32[196]{0:T(256)S(1)}, f32[196]{0:T(256)S(1)}, bf16[512]{0:T(512)(128)(2,1)}, f32[196,512]{1,0:T(8,128)}) fusion(bf16[1,196,512]{2,1,0:T(8,128)(2,1)S(1)} %copy-done.1, f32[196]{0:T(256)S(1)} %add_rsqrt_fusion.1, f32[196]{0:T(256)S(1)} %broadcast_multiply_fusion.5, f32[512]{0:T(512)S(1)} %reshape.370, ...), kind=kOutput, calls=%fused_computation.47 | convolution fusion | flops 309283456 | bytes 2784320 | tf_op jit(solution)/shard_map/dot_general | solution.py:664
  112.3 1.9 fusion.7
  115.0 1.2 fusion.26
  116.3 1.3 convolution_convert_fusion.4
  117.6 1.4 copy.49
  120.7 2.2 %convolution_convert_fusion.1 = bf16[512,2048]{1,0:T(8,128)(2,1)} fusion(bf16[196,2048]{1,0:T(8,128)(2,1)S(1)} %get-tuple-element.118, f32[196,512]{1,0:T(8,128)S(1)} %get-tuple-element.112, f32[512]{0:T(512)S(1)} %copy-done.13, f32[512]{0:T(512)S(1)} %copy-done.9, f32[196]{0:T(256)S(1)} %copy-done.21, f32[196]{0:T(256)S(1)} %copy-done.11), kind=kOutput, calls=%fused_computation.1 | convolution fusion | flops 412592128 | bytes 3307040 | tf_op jit(solution)/shard_map/dot_general | solution.py:647
  123.0 1.9 convolution_convert_fusion.3
  124.9 2.1 %convolution_convert_fusion.2 = bf16[2048,512]{0,1:T(8,128)(2,1)} fusion(bf16[196,2048]{1,0:T(8,128)(2,1)S(1)} %get-tuple-element.113, bf16[1,196,512]{2,1,0:T(8,128)(2,1)S(1)} %copy-done.4), kind=kOutput, calls=%fused_computation.2 | convolution fusion | flops 412090368 | bytes 3100672 | tf_op jit(solution)/shard_map/dot_general | solution.py:643
  127.0 48.2 %scatter_parts.1 = (f32[16,2048]{1,0:T(8,128)}, f32[16,2048]{1,0:T(8,128)}, f32[16,1536]{1,0:T(8,128)}, f32[16,512]{1,0:T(8,128)}, f32[24,128]{1,0:T(8,128)}, /*...) custom-call(bf16[16,2,1,16,2048]{4,3,2,1,0:T(8,128)(2,1)} %bitcast.1, ...), custom_call_target="tpu_custom_call" | custom-call | tf_op jit(solution)/shard_map/scatter_parts/pallas_call | solution.py:404
  178.9 1.5 copy.80
  181.6 1.4 copy.82
  186.4 1.6 copy.86
  189.1 1.6 copy.88
  (149 shorter events, 30.2 us)
Async XLA Ops:
  0.6 9.9 %copy-start = (bf16[169,16]{0,1:T(8,128)(2,1)S(1)}, bf16[169,16]{0,1:T(8,128)(2,1)}, u32[]{:S(2)}) copy-start(bf16[169,16]{0,1:T(8,128)(2,1)} %param.32) | copy-start | bytes 16228
  0.7 11.4 %copy-start.30 = (s32[196]{0:T(256)S(1)}, s32[196]{0:T(256)}, u32[]{:S(2)}) copy-start(s32[196]{0:T(256)} %param.35) | copy-start | bytes 2356
  2.7 105.1 %copy-start.17 = (f32[196]{0:T(256)}, f32[196]{0:T(256)S(1)}, u32[]{:S(2)}) copy-start(f32[196]{0:T(256)S(1)} %broadcast_multiply_fusion.5) | copy-start | bytes 2356
  3.9 104.0 %copy-start.24 = (f32[196]{0:T(256)}, f32[196]{0:T(256)S(1)}, u32[]{:S(2)}) copy-start(f32[196]{0:T(256)S(1)} %add_rsqrt_fusion.1) | copy-start | bytes 2356
  6.3 59.8 %copy-start.22 = (s32[2401]{0:T(1024)}, s32[2401]{0:T(1024)S(1)}, u32[]{:S(2)}) copy-start(s32[2401]{0:T(1024)S(1)} %eq.106) | copy-start | bytes 28816
  10.5 58.5 %copy-start.1 = (bf16[1,196,512]{2,1,0:T(8,128)(2,1)S(1)}, bf16[1,196,512]{2,1,0:T(8,128)(2,1)}, u32[]{:S(2)}) copy-start(bf16[1,196,512]{2,1,0:T(8,128)(2,1)} %param.18) | copy-start | bytes 602116
  68.7 14.1 %copy-start.12 = (f32[512]{0:T(512)}, f32[512]{0:T(512)S(1)}, u32[]{:S(2)}) copy-start(f32[512]{0:T(512)S(1)} %reshape.378) | copy-start | bytes 6148
  68.8 21.5 %copy-start.8 = (f32[512]{0:T(512)}, f32[512]{0:T(512)S(1)}, u32[]{:S(2)}) copy-start(f32[512]{0:T(512)S(1)} %reshape.377) | copy-start | bytes 6148
  69.0 12.4 %copy-start.27 = (f32[512]{0:T(512)}, f32[512]{0:T(512)S(1)}, u32[]{:S(2)}) copy-start(f32[512]{0:T(512)S(1)} %reshape.371) | copy-start | bytes 6148
  69.0 38.8 %copy-start.14 = (f32[512]{0:T(512)}, f32[512]{0:T(512)S(1)}, u32[]{:S(2)}) copy-start(f32[512]{0:T(512)S(1)} %reshape.370) | copy-start | bytes 6148
  82.6 7.7 %copy-start.10 = (f32[196]{0:T(256)}, f32[196]{0:T(256)S(1)}, u32[]{:S(2)}) copy-start(f32[196]{0:T(256)S(1)} %broadcast_multiply_fusion.4) | copy-start | bytes 2356
  82.9 7.5 %copy-start.20 = (f32[196]{0:T(256)}, f32[196]{0:T(256)S(1)}, u32[]{:S(2)}) copy-start(f32[196]{0:T(256)S(1)} %add_rsqrt_fusion) | copy-start | bytes 2356
  107.9 4.3 %copy-start.6 = (f32[16,49,49]{2,1,0:T(8,128)S(1)}, f32[16,49,49]{2,1,0:T(8,128)}, u32[]{:S(2)}) copy-start(f32[16,49,49]{2,1,0:T(8,128)} %get-tuple-element.45) | copy-start | bytes 460996
  107.9 4.4 %copy-start.23 = (s32[2401]{0:T(1024)S(1)}, s32[2401]{0:T(1024)}, u32[]{:S(2)}) copy-start(s32[2401]{0:T(1024)} %copy-done.22) | copy-start | bytes 28816
  115.0 4.2 %copy-start.38 = (bf16[512]{0:T(512)(128)(2,1)S(1)}, bf16[512]{0:T(512)(128)(2,1)}, u32[]{:S(2)}) copy-start(bf16[512]{0:T(512)(128)(2,1)} %get-tuple-element.93) | copy-start | bytes 3076
  115.0 4.3 %copy-start.31 = (bf16[512]{0:T(512)(128)(2,1)S(1)}, bf16[512]{0:T(512)(128)(2,1)}, u32[]{:S(2)}) copy-start(bf16[512]{0:T(512)(128)(2,1)} %get-tuple-element.101) | copy-start | bytes 3076
  115.0 4.4 %copy-start.36 = (bf16[512]{0:T(512)(128)(2,1)S(1)}, bf16[512]{0:T(512)(128)(2,1)}, u32[]{:S(2)}) copy-start(bf16[512]{0:T(512)(128)(2,1)} %get-tuple-element.89) | copy-start | bytes 3076
  115.0 4.5 %copy-start.37 = (bf16[512]{0:T(512)(128)(2,1)S(1)}, bf16[512]{0:T(512)(128)(2,1)}, u32[]{:S(2)}) copy-start(bf16[512]{0:T(512)(128)(2,1)} %get-tuple-element.97) | copy-start | bytes 3076
  115.0 4.6 %copy-start.35 = (bf16[512]{0:T(512)(128)(2,1)S(1)}, bf16[512]{0:T(512)(128)(2,1)}, u32[]{:S(2)}) copy-start(bf16[512]{0:T(512)(128)(2,1)} %get-tuple-element.98) | copy-start | bytes 3076
  115.0 4.6 %copy-start.7 = (bf16[32,1,16]{2,0,1:T(8,128)(2,1)S(1)}, bf16[32,1,16]{2,0,1:T(8,128)(2,1)}, u32[]{:S(2)}) copy-start(bf16[32,1,16]{2,0,1:T(8,128)(2,1)} %broadcast_in_dim_reshape.2) | copy-start | bytes 3076
  116.2 4.4 %copy-start.9 = (f32[512]{0:T(512)S(1)}, f32[512]{0:T(512)}, u32[]{:S(2)}) copy-start(f32[512]{0:T(512)} %copy-done.8) | copy-start | bytes 6148
  116.3 4.4 %copy-start.11 = (f32[196]{0:T(256)S(1)}, f32[196]{0:T(256)}, u32[]{:S(2)}) copy-start(f32[196]{0:T(256)} %copy-done.10) | copy-start | bytes 2356
  116.3 4.4 %copy-start.13 = (f32[512]{0:T(512)S(1)}, f32[512]{0:T(512)}, u32[]{:S(2)}) copy-start(f32[512]{0:T(512)} %copy-done.12) | copy-start | bytes 6148
  116.3 4.4 %copy-start.21 = (f32[196]{0:T(256)S(1)}, f32[196]{0:T(256)}, u32[]{:S(2)}) copy-start(f32[196]{0:T(256)} %copy-done.20) | copy-start | bytes 2356
  (15 other events, 44.4 us)

commit v3 on v2

--- a/solution.py
+++ b/solution.py
@@ -386,6 +386,25 @@
     return (1 << (len(left) - 1 - place_of), 2, 1 << place_of)
 
 
+def settle_kernel(*refs):
+    half = len(refs) // 2
+    for source, target in zip(refs[:half], refs[half:]):
+        target[...] = source[...]
+
+
+def settle(arrays):
+    spec = pl.BlockSpec(memory_space=pltpu.VMEM)
+    return list(
+        pl.pallas_call(
+            settle_kernel,
+            out_shape=[jax.ShapeDtypeStruct(a.shape, a.dtype) for a in arrays],
+            in_specs=[spec] * len(arrays),
+            out_specs=[spec] * len(arrays),
+            name="settle",
+        )(*arrays)
+    )
+
+
 def scatter_parts(parts, table, count, split, lengths):
     bit_count = count.bit_length() - 1
     part_count = len(parts)
@@ -424,6 +443,7 @@
         compiler_params=pltpu.CompilerParams(collective_id=1, has_side_effects=True),
         name="scatter_parts",
     )(*shaped, table)
+    outs = settle(outs)
     return (outs[:part_count], outs[part_count + 1 :], outs[part_count])
 
 

time: 193 us -> 179 us (0.927)
  local copies, waits for them, and re-layouts: 26.7 us -> 11.6 us
    unnamed x92 -> x80, local copies, waits for them, and re-layouts: 17.4 us -> 2.29 us
where the time goes in v3:
time: 179 us
  Pallas kernels  126 us (70%)
  matrix products  26 us (15%)
  other arithmetic  13.2 us (7%)
  local copies, waits for them, and re-layouts  11.6 us (6%)
    pallas_call x1, Pallas kernels, gather_parts(): pl.pallas_call(functools.partial(gather_kernel, bit_count, part_count), o...  51.2 us
    pallas_call x1, Pallas kernels, scatter_parts(): pl.pallas_call(functools.partial(scatter_kernel, bit_count, part_count, s...  48.2 us
    pallas_call x1, Pallas kernels, attend_back(): pl.pallas_call(functools.partial(attend_back_kernel, model // HEADS), out...  15.7 us
    pallas_call x1, Pallas kernels, attend(): pl.pallas_call(functools.partial(attend_kernel, model // HEADS), out_shap...  9.45 us
    dot_general x1, matrix products, backward_pass(): jnp.dot(qkv_grad_b, qkv_weight.T, preferred_element_type=jnp.float32)  3.62 us

profile of v3, /device:TPU:0, one launch (start us, length us, event | category | flops | bytes accessed | tf_op | source)
XLA Modules:
  0.0 178.5 jit_solution(14470911136930298031)
XLA Ops:
  1.7 1.0 convert_reduce_fusion
  2.7 1.1 fusion.30
  6.3 1.3 pad_maximum_fusion.1.refs_3_
  12.8 51.2 %gather_parts.1 = (bf16[2,2,2,2,2,16,2048]{6,5,4,3,2,1,0:T(8,128)(2,1)}, bf16[2,2,2,2,2,16,2048]{6,5,4,3,2,1,0:T(8,128)(2,1)}, bf16[2,2,2,2,2,16,1536]{6,5,4,3,2...) custom-call(bf16[16,2048]{1,0:T(8,128)(2,1)} %refs_0_.1, bf16[16,2048]{1,0:T(8,128)(2,1)} %bitcast.143, ...), custom_call_target="tpu_custom_call" | custom-call | tf_op jit(solution)/shard_map/gather_parts/pallas_call | solution.py:274
  66.1 1.4 fusion.76
  67.4 1.1 slice.69
  69.1 2.8 %fusion.1.qkv_ref = bf16[196,1536]{1,0:T(8,128)(2,1)} fusion(bf16[512,1536]{1,0:T(8,128)(2,1)} %bitcast.152, f32[1536]{0:T(1024)S(1)} %pad_maximum_fusion.2, bf16[1,196,512]{2,1,0:T(8,128)(2,1)S(1)} %copy-done.1, f32[512]{0:T(512)S(1)} %reshape.371, f32[512]{0:T(512)S(1)} %reshape.370, f32[196]{0:T(256)S(1)} %add_rsqrt_fusion.1, ...), kind=kOutput, calls=%fused_computation.8 | convolution fusion | flops 309485568 | bytes 2387488 | tf_op jit(solution)/shard_map/dot_general | solution.py:595
  71.9 9.5 %attend.1 = (bf16[196,1536]{1,0:T(8,128)(2,1)}, bf16[196,512]{1,0:T(8,128)(2,1)}) custom-call(bf16[196,1536]{1,0:T(8,128)(2,1)} %fusion.1.qkv_ref, bf16[196,196]{1,0:T(8,128)(2,1)} %get-tuple-element.136.pick_ref, bf16[196,196]{1,0:T(8,128)(2,1)} %get-tuple-element.135.back_ref, bf16[16,49,49]{2,1,0:T(8,128)(2,1)} %bitcast.135, ...), custom_call_target="tpu_custom_call" | custom-call | tf_op jit(solution)/shard_map/attend/pallas_call | solution.py:170
  81.3 1.3 fusion.77
  82.9 2.6 %multiply_convert_fusion = (bf16[196,2048]{1,0:T(8,128)(2,1)S(1)}, f32[196,2048]{1,0:T(8,128)S(1)}) fusion(f32[2048]{0:T(1024)S(1)} %reshape.379, bf16[512,2048]{1,0:T(8,128)(2,1)} %bitcast.130, f32[196,512]{1,0:T(8,128)S(1)} %get-tuple-element.138, f32[512]{0:T(512)S(1)} %reshape.378, f32[512]{0:T(512)S(1)} %reshape.377, f32[196]{0:T(256)S(1)} %add_rsqrt_fusion, ...), kind=kOutput, calls=%fused_computation.16 | convolution fusion | flops 413952000 | bytes 4920864 | tf_op jit(solution)/shard_map/dot_general | solution.py:607
  85.5 1.8 fusion.78
  87.2 1.5 fusion.14
  88.8 1.5 multiply_reduce_fusion
  92.1 15.7 %attend_back.1 = (bf16[196,1536]{1,0:T(8,128)(2,1)}, f32[1,1536]{1,0:T(1,128)}, f32[16,49,49]{2,1,0:T(8,128)}) custom-call(bf16[196,1536]{1,0:T(8,128)(2,1)} %get-tuple-element.55.qkv_win_ref, bf16[196,512]{1,0:T(8,128)(2,1)} %convolution_convert_fusion.5.grad_ref, bf16[196,196]{1,0:T(8,128)(2,1)} %get-tuple-element.136.pick_ref, ...), custom_call_target="tpu_custom_call" | custom-call | tf_op jit(solution)/shard_map/attend_back/pallas_call | solution.py:187
  107.9 3.6 %fusion.29 = (bf16[512]{0:T(512)(128)(2,1)}, f32[196]{0:T(256)S(1)}, f32[196]{0:T(256)S(1)}, bf16[512]{0:T(512)(128)(2,1)}, f32[196,512]{1,0:T(8,128)}) fusion(bf16[1,196,512]{2,1,0:T(8,128)(2,1)S(1)} %copy-done.1, f32[196]{0:T(256)S(1)} %add_rsqrt_fusion.1, f32[196]{0:T(256)S(1)} %broadcast_multiply_fusion.5, f32[512]{0:T(512)S(1)} %reshape.370, ...), kind=kOutput, calls=%fused_computation.47 | convolution fusion | flops 309283456 | bytes 2784320 | tf_op jit(solution)/shard_map/dot_general | solution.py:684
  112.3 1.9 %fusion.7 = f32[169,16]{1,0:T(8,128)S(1)} fusion(f32[2401,16]{0,1:T(8,128)S(1)} %reshape.367, s32[2401]{0:T(1024)S(1)} %copy-done.23), kind=kOutput, calls=%fused_computation.19 | convolution fusion | flops 78719184 | bytes 174084 | tf_op jit(solution)/shard_map/dot_general | solution.py:766
  115.0 1.2 fusion.26
  116.3 1.3 convolution_convert_fusion.4
  117.6 1.4 copy.49
  120.7 2.2 %convolution_convert_fusion.1 = bf16[512,2048]{1,0:T(8,128)(2,1)} fusion(bf16[196,2048]{1,0:T(8,128)(2,1)S(1)} %get-tuple-element.144, f32[196,512]{1,0:T(8,128)S(1)} %get-tuple-element.138, f32[512]{0:T(512)S(1)} %copy-done.13, f32[512]{0:T(512)S(1)} %copy-done.9, f32[196]{0:T(256)S(1)} %copy-done.21, f32[196]{0:T(256)S(1)} %copy-done.11), kind=kOutput, calls=%fused_computation.1 | convolution fusion | flops 412592128 | bytes 3307040 | tf_op jit(solution)/shard_map/dot_general | solution.py:667
  123.0 1.9 %convolution_convert_fusion.3 = bf16[512,1536]{1,0:T(8,128)(2,1)} fusion(bf16[196,1536]{1,0:T(8,128)(2,1)S(1)} %copy-done.5, bf16[1,196,512]{2,1,0:T(8,128)(2,1)S(1)} %copy-done.1, f32[512]{0:T(512)S(1)} %copy-done.28, f32[512]{0:T(512)S(1)} %copy-done.16, f32[196]{0:T(256)S(1)} %copy-done.26, f32[196]{0:T(256)S(1)} %copy-done.19), kind=kOutput, calls=%fused_computation.3 | convolution fusion | flops 309669888 | bytes 2381344 | tf_op jit(solution)/shard_map/dot_general | solution.py:682
  124.9 2.1 %convolution_convert_fusion.2 = bf16[2048,512]{0,1:T(8,128)(2,1)} fusion(bf16[196,2048]{1,0:T(8,128)(2,1)S(1)} %get-tuple-element.139, bf16[1,196,512]{2,1,0:T(8,128)(2,1)S(1)} %copy-done.4), kind=kOutput, calls=%fused_computation.2 | convolution fusion | flops 412090368 | bytes 3100672 | tf_op jit(solution)/shard_map/dot_general | solution.py:663
  127.0 48.2 %scatter_parts.1 = (f32[16,2048]{1,0:T(8,128)}, f32[16,2048]{1,0:T(8,128)}, f32[16,1536]{1,0:T(8,128)}, f32[16,512]{1,0:T(8,128)}, f32[24,128]{1,0:T(8,128)}, /*...) custom-call(bf16[16,2,1,16,2048]{4,3,2,1,0:T(8,128)(2,1)} %bitcast.1, ...), custom_call_target="tpu_custom_call" | custom-call | tf_op jit(solution)/shard_map/scatter_parts/pallas_call | solution.py:423
  175.2 1.9 %settle.1 = (f32[16,2048]{1,0:T(8,128)}, f32[16,2048]{1,0:T(8,128)}, f32[16,1536]{1,0:T(8,128)}, f32[16,512]{1,0:T(8,128)}, f32[24,128]{1,0:T(8,128)}, /*index=5...) custom-call(f32[16,2048]{1,0:T(8,128)} %get-tuple-element.59.refs_0_, ...), custom_call_target="tpu_custom_call" | custom-call | tf_op jit(solution)/shard_map/settle/pallas_call | solution.py:398
  (138 shorter events, 17.9 us)
Async XLA Ops:
  0.6 9.9 %copy-start = (bf16[169,16]{0,1:T(8,128)(2,1)S(1)}, bf16[169,16]{0,1:T(8,128)(2,1)}, u32[]{:S(2)}) copy-start(bf16[169,16]{0,1:T(8,128)(2,1)} %param.32) | copy-start | bytes 16228
  0.7 11.4 %copy-start.30 = (s32[196]{0:T(256)S(1)}, s32[196]{0:T(256)}, u32[]{:S(2)}) copy-start(s32[196]{0:T(256)} %param.35) | copy-start | bytes 2356
  2.7 105.1 %copy-start.17 = (f32[196]{0:T(256)}, f32[196]{0:T(256)S(1)}, u32[]{:S(2)}) copy-start(f32[196]{0:T(256)S(1)} %broadcast_multiply_fusion.5) | copy-start | bytes 2356
  3.9 104.0 %copy-start.24 = (f32[196]{0:T(256)}, f32[196]{0:T(256)S(1)}, u32[]{:S(2)}) copy-start(f32[196]{0:T(256)S(1)} %add_rsqrt_fusion.1) | copy-start | bytes 2356
  6.3 59.8 %copy-start.22 = (s32[2401]{0:T(1024)}, s32[2401]{0:T(1024)S(1)}, u32[]{:S(2)}) copy-start(s32[2401]{0:T(1024)S(1)} %eq.106) | copy-start | bytes 28816
  10.5 58.5 %copy-start.1 = (bf16[1,196,512]{2,1,0:T(8,128)(2,1)S(1)}, bf16[1,196,512]{2,1,0:T(8,128)(2,1)}, u32[]{:S(2)}) copy-start(bf16[1,196,512]{2,1,0:T(8,128)(2,1)} %param.18) | copy-start | bytes 602116
  68.7 14.1 %copy-start.12 = (f32[512]{0:T(512)}, f32[512]{0:T(512)S(1)}, u32[]{:S(2)}) copy-start(f32[512]{0:T(512)S(1)} %reshape.378) | copy-start | bytes 6148
  68.8 21.5 %copy-start.8 = (f32[512]{0:T(512)}, f32[512]{0:T(512)S(1)}, u32[]{:S(2)}) copy-start(f32[512]{0:T(512)S(1)} %reshape.377) | copy-start | bytes 6148
  69.0 12.4 %copy-start.27 = (f32[512]{0:T(512)}, f32[512]{0:T(512)S(1)}, u32[]{:S(2)}) copy-start(f32[512]{0:T(512)S(1)} %reshape.371) | copy-start | bytes 6148
  69.0 38.8 %copy-start.14 = (f32[512]{0:T(512)}, f32[512]{0:T(512)S(1)}, u32[]{:S(2)}) copy-start(f32[512]{0:T(512)S(1)} %reshape.370) | copy-start | bytes 6148
  82.6 7.7 %copy-start.10 = (f32[196]{0:T(256)}, f32[196]{0:T(256)S(1)}, u32[]{:S(2)}) copy-start(f32[196]{0:T(256)S(1)} %broadcast_multiply_fusion.4) | copy-start | bytes 2356
  82.9 7.5 %copy-start.20 = (f32[196]{0:T(256)}, f32[196]{0:T(256)S(1)}, u32[]{:S(2)}) copy-start(f32[196]{0:T(256)S(1)} %add_rsqrt_fusion) | copy-start | bytes 2356
  107.9 4.3 %copy-start.6 = (f32[16,49,49]{2,1,0:T(8,128)S(1)}, f32[16,49,49]{2,1,0:T(8,128)}, u32[]{:S(2)}) copy-start(f32[16,49,49]{2,1,0:T(8,128)} %get-tuple-element.58) | copy-start | bytes 460996
  107.9 4.4 %copy-start.23 = (s32[2401]{0:T(1024)S(1)}, s32[2401]{0:T(1024)}, u32[]{:S(2)}) copy-start(s32[2401]{0:T(1024)} %copy-done.22) | copy-start | bytes 28816
  115.0 4.2 %copy-start.38 = (bf16[512]{0:T(512)(128)(2,1)S(1)}, bf16[512]{0:T(512)(128)(2,1)}, u32[]{:S(2)}) copy-start(bf16[512]{0:T(512)(128)(2,1)} %get-tuple-element.119) | copy-start | bytes 3076
  115.0 4.3 %copy-start.31 = (bf16[512]{0:T(512)(128)(2,1)S(1)}, bf16[512]{0:T(512)(128)(2,1)}, u32[]{:S(2)}) copy-start(bf16[512]{0:T(512)(128)(2,1)} %get-tuple-element.127) | copy-start | bytes 3076
  115.0 4.4 %copy-start.36 = (bf16[512]{0:T(512)(128)(2,1)S(1)}, bf16[512]{0:T(512)(128)(2,1)}, u32[]{:S(2)}) copy-start(bf16[512]{0:T(512)(128)(2,1)} %get-tuple-element.115) | copy-start | bytes 3076
  115.0 4.5 %copy-start.37 = (bf16[512]{0:T(512)(128)(2,1)S(1)}, bf16[512]{0:T(512)(128)(2,1)}, u32[]{:S(2)}) copy-start(bf16[512]{0:T(512)(128)(2,1)} %get-tuple-element.123) | copy-start | bytes 3076
  115.0 4.6 %copy-start.35 = (bf16[512]{0:T(512)(128)(2,1)S(1)}, bf16[512]{0:T(512)(128)(2,1)}, u32[]{:S(2)}) copy-start(bf16[512]{0:T(512)(128)(2,1)} %get-tuple-element.124) | copy-start | bytes 3076
  115.0 4.6 %copy-start.7 = (bf16[32,1,16]{2,0,1:T(8,128)(2,1)S(1)}, bf16[32,1,16]{2,0,1:T(8,128)(2,1)}, u32[]{:S(2)}) copy-start(bf16[32,1,16]{2,0,1:T(8,128)(2,1)} %broadcast_in_dim_reshape.2) | copy-start | bytes 3076
  116.2 4.4 %copy-start.9 = (f32[512]{0:T(512)S(1)}, f32[512]{0:T(512)}, u32[]{:S(2)}) copy-start(f32[512]{0:T(512)} %copy-done.8) | copy-start | bytes 6148
  116.3 4.4 %copy-start.11 = (f32[196]{0:T(256)S(1)}, f32[196]{0:T(256)}, u32[]{:S(2)}) copy-start(f32[196]{0:T(256)} %copy-done.10) | copy-start | bytes 2356
  116.3 4.4 %copy-start.13 = (f32[512]{0:T(512)S(1)}, f32[512]{0:T(512)}, u32[]{:S(2)}) copy-start(f32[512]{0:T(512)} %copy-done.12) | copy-start | bytes 6148
  116.3 4.4 %copy-start.21 = (f32[196]{0:T(256)S(1)}, f32[196]{0:T(256)}, u32[]{:S(2)}) copy-start(f32[196]{0:T(256)} %copy-done.20) | copy-start | bytes 2356
  (15 other events, 44.4 us)
